TPU v7x, 32 devices: a whole 2x2x4 slice. The times are simulated.
32 devices in a mesh: lat: 4 (over y, x), lon: 8 (over z, core).
Axes of the slice: x: 2, y: 2, z: 4, core: 2. Of those that a mesh axis runs over, the one named last changes fastest.
Arguments:
- queries: bfloat16 [64, 64, 768], P('lat', 'lon'), may hold values from -8 to 8
- key_vectors: bfloat16 [64, 64, 768], P('lat', 'lon'), may hold values from -8 to 8
- value_vectors: bfloat16 [64, 64, 768], P('lat', 'lon'), may hold values from -12 to 12
- upstream: bfloat16 [64, 64, 768], P('lat', 'lon'), may hold values from -6 to 6
- w_out: bfloat16 [768, 768], replicated, may hold values from -0.21875 to 0.21875
- neighbours: int32 [8, 8, 4], replicated, may hold values from 0 to 63, as said below
- counts: int32 [8, 8], replicated, may hold values from 2 to 4, as said below
Outputs:
- mixed_out: bfloat16 [64, 64, 768], P('lat', 'lon')
- q_grad: bfloat16 [64, 64, 768], P('lat', 'lon')
- k_grad: bfloat16 [64, 64, 768], P('lat', 'lon')
- v_grad: bfloat16 [64, 64, 768], P('lat', 'lon')
- w_grad: float32 [768, 768], replicated
Inputs may be any that keep to these rules, and one draw needn't show every extreme that they name: `neighbours`: entry s of block (i, j) names a block i2 * 8 + j2 with i2 within one of i and j2 within one of j around the longitude circle; slot 0 names the block itself, the entries of slots below counts[i, j] are distinct, and the slots at or beyond counts[i, j] name the block itself. `counts`: every block outside the first and the last row of blocks has 4.
All inputs are finite; a program needn't handle non-finite values.
Results may differ from a plain program's by a relative error of at most 0.03.
Values may be sent and summed in bfloat16 or wider, within the bound.
No kernel may reach another device: no remote copies, remote signals or barrier semaphores. Data moves between devices by JAX's collectives and lax.ppermute only.
A program may use at most 64 MiB of HBM per device.

v0:
```python
import math

import jax
import jax.numpy as jnp
from jax import lax
from jax.sharding import PartitionSpec as P

HEADS = 12
HEAD_DIM = 64
BLK = 8
SLOTS = 4


def padded_2(value, sides, width):
    for axis, dim in sides:
        peers, length = (lax.axis_size(axis), value.shape[dim])
        up = [(i, (i + 1) % peers) for i in range(peers)]
        down = [(j, i) for i, j in up]
        last = lax.slice_in_dim(value, length - width, length, axis=dim)
        leading = lax.slice_in_dim(value, 0, width, axis=dim)
        before = lax.ppermute(last, axis, up)
        after = lax.ppermute(leading, axis, down)
        value = jnp.concatenate([before, value, after], axis=dim)
    return value


def to_blocks(token_grid):
    lat_rows, lon_cols, feat_width = token_grid.shape
    block_tiles = token_grid.reshape(
        lat_rows // BLK, BLK, lon_cols // BLK, BLK, feat_width
    ).transpose(0, 2, 1, 3, 4)
    return block_tiles.reshape(lat_rows // BLK * (lon_cols // BLK), BLK * BLK, feat_width)


def from_blocks(block_tiles, lat_blocks, lon_blocks):
    feat_width = block_tiles.shape[-1]
    token_grid = block_tiles.reshape(lat_blocks, lon_blocks, BLK, BLK, feat_width).transpose(
        0, 2, 1, 3, 4
    )
    return token_grid.reshape(lat_blocks * BLK, lon_blocks * BLK, feat_width)


def split_heads(block_tiles):
    return block_tiles.reshape(block_tiles.shape[0], block_tiles.shape[1], HEADS, HEAD_DIM)


def slot_places(
    neighbours,
    counts,
    first_lat,
    first_lon,
    grid_rows,
    grid_cols,
    anchor_lat,
    anchor_lon,
    pad_rows,
    pad_cols,
):
    total_lat = neighbours.shape[0]
    total_lon = neighbours.shape[1]
    block_lat = first_lat + jnp.arange(grid_rows, dtype=jnp.int32)
    block_lon = (first_lon + jnp.arange(grid_cols, dtype=jnp.int32)) % total_lon
    inside = (block_lat >= 0) & (block_lat < total_lat)
    safe_lat = jnp.clip(block_lat, 0, total_lat - 1)
    slot_table = jnp.take(jnp.take(neighbours, safe_lat, axis=0), block_lon, axis=1)
    slot_limit = jnp.take(jnp.take(counts, safe_lat, axis=0), block_lon, axis=1)
    slot_ids = jnp.arange(SLOTS, dtype=jnp.int32)
    rel_lat = slot_table // total_lon - anchor_lat
    rel_lon = (slot_table % total_lon - anchor_lon) % total_lon
    usable = (slot_ids[None, None, :] < slot_limit[:, :, None]) & inside[:, None, None]
    usable = usable & (rel_lat >= 0) & (rel_lat < pad_rows) & (rel_lon < pad_cols)
    key_place = jnp.where(usable, rel_lat * pad_cols + rel_lon, 0)
    return (
        key_place.reshape(grid_rows * grid_cols, SLOTS),
        usable.reshape(grid_rows * grid_cols, SLOTS),
    )


def gather_sets(padded_tiles, key_place):
    picked = jnp.take(padded_tiles, key_place.reshape(-1), axis=0)
    return picked.reshape(key_place.shape[0], SLOTS * BLK * BLK, padded_tiles.shape[-1])


def masked_scores(query_tiles, key_sets, key_valid):
    raw = jnp.einsum(
        "nqhd,nkhd->nhqk",
        split_heads(query_tiles),
        split_heads(key_sets),
        preferred_element_type=jnp.float32,
    )
    raw = raw * (1.0 / math.sqrt(HEAD_DIM))
    return jnp.where(key_valid[:, None, None, :], raw, -jnp.inf)


def forward_core(query_tiles, key_sets, value_sets, key_valid):
    masked = masked_scores(query_tiles, key_sets, key_valid)
    row_top = jnp.max(masked, axis=-1, keepdims=True)
    exp_total = jnp.sum(jnp.exp(masked - row_top), axis=-1, keepdims=True)
    log_total = row_top + jnp.log(exp_total)
    attn_probs = jnp.exp(masked - log_total)
    probs_low = attn_probs.astype(jnp.bfloat16)
    mixed_heads = jnp.einsum(
        "nhqk,nkhd->nqhd", probs_low, split_heads(value_sets), preferred_element_type=jnp.float32
    )
    attended = mixed_heads.astype(jnp.bfloat16).reshape(query_tiles.shape)
    return (attended, attn_probs, probs_low, log_total[..., 0])


def head_delta(d_att, attended):
    product = d_att.astype(jnp.float32) * attended.astype(jnp.float32)
    return jnp.sum(split_heads(product), axis=-1).transpose(0, 2, 1)


def backward_scores(attn_probs, d_att, row_delta, value_sets):
    dprobs = jnp.einsum(
        "nqhd,nkhd->nhqk",
        split_heads(d_att),
        split_heads(value_sets),
        preferred_element_type=jnp.float32,
    )
    return (attn_probs * (dprobs - row_delta[..., None]) * (1.0 / math.sqrt(HEAD_DIM))).astype(
        jnp.bfloat16
    )


def grad_queries(dscores, key_sets):
    summed = jnp.einsum(
        "nhqk,nkhd->nqhd", dscores, split_heads(key_sets), preferred_element_type=jnp.float32
    )
    return summed.astype(jnp.bfloat16).reshape(summed.shape[0], summed.shape[1], -1)


def contract_keys(weights_low, block_tiles):
    summed = jnp.einsum(
        "nhqk,nqhd->nkhd", weights_low, split_heads(block_tiles), preferred_element_type=jnp.float32
    )
    return summed.reshape(summed.shape[0], summed.shape[1], -1)


def add_into(contrib, key_place, usable, pad_count):
    flat_place = key_place.reshape(-1)
    feat_width = contrib.shape[-1]
    flat_terms = contrib.reshape(flat_place.shape[0], BLK * BLK * feat_width)
    flat_terms = jnp.where(usable.reshape(-1)[:, None], flat_terms, 0.0)
    summed = (
        jnp.zeros((pad_count, BLK * BLK * feat_width), jnp.float32).at[flat_place].add(flat_terms)
    )
    return summed.reshape(pad_count, BLK * BLK, feat_width)


def fold_joint(extended, lat_rows, lon_cols):
    low_lat = lat_rows + 3 * BLK
    low_lon = lon_cols + 3 * BLK
    interior = extended[:, 2 * BLK : 2 * BLK + lat_rows, 2 * BLK : 2 * BLK + lon_cols]
    interior = interior.at[:, :BLK, :].add(extended[:, :BLK, 2 * BLK : 2 * BLK + lon_cols])
    interior = interior.at[:, lat_rows - BLK :, :].add(
        extended[:, low_lat:, 2 * BLK : 2 * BLK + lon_cols]
    )
    interior = interior.at[:, :, :BLK].add(extended[:, 2 * BLK : 2 * BLK + lat_rows, :BLK])
    interior = interior.at[:, :, lon_cols - BLK :].add(
        extended[:, 2 * BLK : 2 * BLK + lat_rows, low_lon:]
    )
    interior = interior.at[:, :BLK, :BLK].add(extended[:, :BLK, :BLK])
    interior = interior.at[:, :BLK, lon_cols - BLK :].add(extended[:, :BLK, low_lon:])
    interior = interior.at[:, lat_rows - BLK :, :BLK].add(extended[:, low_lat:, :BLK])
    return interior.at[:, lat_rows - BLK :, lon_cols - BLK :].add(extended[:, low_lat:, low_lon:])


def on_device(queries, key_vectors, value_vectors, upstream, w_out, neighbours, counts):
    lat_rows, lon_cols, feat_width = queries.shape
    lat_blocks = lat_rows // BLK
    lon_blocks = lon_cols // BLK
    pad_rows = lat_blocks + 2
    pad_cols = lon_blocks + 2
    pad_count = pad_rows * pad_cols
    inner_count = BLK * BLK
    tokens_all = lat_rows * lon_cols * lax.axis_size("lat") * lax.axis_size("lon")
    first_lat = lax.axis_index("lat") * lat_blocks
    first_lon = lax.axis_index("lon") * lon_blocks
    stacked = jnp.stack((key_vectors, value_vectors))
    padded = padded_2(stacked, (("lat", 1), ("lon", 2)), BLK)
    key_tiles = to_blocks(padded[0])
    value_tiles = to_blocks(padded[1])
    own_place, own_usable = slot_places(
        neighbours,
        counts,
        first_lat,
        first_lon,
        lat_blocks,
        lon_blocks,
        first_lat - 1,
        first_lon - 1,
        pad_rows,
        pad_cols,
    )
    query_tiles = to_blocks(queries)
    key_sets = gather_sets(key_tiles, own_place)
    value_sets = gather_sets(value_tiles, own_place)
    key_valid = jnp.repeat(own_usable, inner_count, axis=1)
    attended, attn_probs, probs_low, log_total = forward_core(
        query_tiles, key_sets, value_sets, key_valid
    )
    flat_att = attended.reshape(-1, feat_width)
    mixed_flat = jnp.dot(flat_att, w_out, preferred_element_type=jnp.float32).astype(jnp.bfloat16)
    grad_tiles = to_blocks(upstream)
    flat_grad = grad_tiles.reshape(-1, feat_width)
    local_weight = lax.dot_general(
        flat_att, flat_grad, (((0,), (0,)), ((), ())), preferred_element_type=jnp.float32
    )
    w_grad = lax.psum(local_weight, ("lat", "lon")) / math.sqrt(tokens_all)
    d_att = lax.dot_general(
        flat_grad, w_out, (((1,), (1,)), ((), ())), preferred_element_type=jnp.float32
    )
    d_att = d_att.astype(jnp.bfloat16).reshape(attended.shape)
    row_delta = head_delta(d_att, attended)
    dscores = backward_scores(attn_probs, d_att, row_delta, value_sets)
    query_grad = grad_queries(dscores, key_sets)
    key_contrib = contract_keys(dscores, query_tiles)
    value_contrib = contract_keys(probs_low, d_att)
    key_pad = from_blocks(
        add_into(key_contrib, own_place, own_usable, pad_count), pad_rows, pad_cols
    )
    value_pad = from_blocks(
        add_into(value_contrib, own_place, own_usable, pad_count), pad_rows, pad_cols
    )
    pad_terms = jnp.stack((key_pad, value_pad))
    extended = padded_2(pad_terms.astype(jnp.bfloat16), (("lat", 1), ("lon", 2)), BLK).astype(
        pad_terms.dtype
    )
    folded = fold_joint(extended, lat_rows, lon_cols)
    key_grad = folded[0].astype(jnp.bfloat16)
    value_grad = folded[1].astype(jnp.bfloat16)
    mixed_out = from_blocks(mixed_flat.reshape(attended.shape), lat_blocks, lon_blocks)
    q_grad = from_blocks(query_grad, lat_blocks, lon_blocks)
    return (mixed_out, q_grad, key_grad, value_grad, w_grad)


def solution(mesh):
    return jax.shard_map(
        on_device,
        mesh=mesh,
        in_specs=(
            P("lat", "lon", None),
            P("lat", "lon", None),
            P("lat", "lon", None),
            P("lat", "lon", None),
            P(),
            P(),
            P(),
        ),
        out_specs=(
            P("lat", "lon", None),
            P("lat", "lon", None),
            P("lat", "lon", None),
            P("lat", "lon", None),
            P(),
        ),
        check_vma=False,
    )
```

profile of v0, /device:TPU:0, one launch (start us, length us, event | category | flops | bytes accessed | tf_op | source)
XLA Modules:
  0.0 270.1 jit_solution(14660080153096011954)
XLA Ops:
  8.4 4.0 %collective-permute-start.1 = (bf16[2,8,8,768]{3,2,1,0:T(8,128)(2,1)S(1)}, bf16[2,8,8,768]{3,2,1,0:T(8,128)(2,1)S(1)}, u32[]{:S(2)}, u32[]{:S(2)}) collective-permute-start(bf16[2,8,8,768]{3,2,1,0:T(8,128)(2,1)S(1)} %get-tuple-element.152), channel_id=1, source_target_pairs={{8,0},{16,8},{24,16},{0,24},{9,1},{17,9},{25,17},{1,25},{10,2},{18... | collective-permute-start | bytes 589832 | tf_op jit(solution)/shard_map/ppermute | solution.py:22
  17.7 4.1 %collective-permute-done = bf16[2,8,8,768]{3,2,1,0:T(8,128)(2,1)S(1)} collective-permute-done((bf16[2,8,8,768]{3,2,1,0:T(8,128)(2,1)S(1)}, bf16[2,8,8,768]{3,2,1,0:T(8,128)(2,1)S(1)}, u32[]{:S(2)}, u32[]{:S(2)}) %collective-permute-start) | collective-permute-done | bytes 196640 | tf_op jit(solution)/shard_map/ppermute | solution.py:21
  22.8 2.2 collective-permute-start.3
  30.0 12.1 %collective-permute-done.3 = bf16[2,32,8,768]{3,2,1,0:T(8,128)(2,1)S(1)} collective-permute-done((bf16[2,32,8,768]{3,2,1,0:T(8,128)(2,1)}, bf16[2,32,8,768]{3,2,1,0:T(8,128)(2,1)S(1)}, u32[]{:S(2)}, u32[]{:S(2)}) %collective-permute-start.3) | collective-permute-done | bytes 786464 | tf_op jit(solution)/shard_map/ppermute | solution.py:22
  42.1 3.0 %collective-permute-done.2 = bf16[2,32,8,768]{3,2,1,0:T(8,128)(2,1)} collective-permute-done((bf16[2,32,8,768]{3,2,1,0:T(8,128)(2,1)}, bf16[2,32,8,768]{3,2,1,0:T(8,128)(2,1)}, u32[]{:S(2)}, u32[]{:S(2)}) %collective-permute-start.2) | collective-permute-done | bytes 786464 | tf_op jit(solution)/shard_map/ppermute | solution.py:21
  48.2 1.5 gather_fusion.2
  49.7 2.5 broadcast_select_fusion.2
  52.2 2.7 %reshape.774 = bf16[2,256,12,64]{3,2,1,0:T(8,128)(2,1)S(1)} reshape(bf16[8,64,768]{2,1,0:T(8,128)(2,1)} %get-tuple-element.156) | data formatting | bytes 1572864 | tf_op jit(solution)/shard_map/reshape;reshape | solution.py:44
  54.9 2.1 copy.37
  57.1 2.7 %reshape.775 = bf16[2,256,12,64]{3,2,1,0:T(8,128)(2,1)S(1)} reshape(bf16[8,64,768]{2,1,0:T(8,128)(2,1)} %get-tuple-element.155) | data formatting | bytes 1572864 | tf_op jit(solution)/shard_map/reshape;reshape | solution.py:44
  59.8 2.1 copy.35
  62.0 1.8 bitcast_reduce_fusion
  69.9 4.7 %copy.46 = f32[2,256,12,64]{3,2,1,0:T(8,128)} copy(f32[2,256,12,64]{1,3,2,0:T(8,128)} %convolution_bitcast_fusion) | data formatting | bytes 3145728 | tf_op jit(solution)/shard_map/nhqk,nqhd->nkhd/transpose | solution.py:134
  74.6 4.4 %reshape_reshape.37 = f32[8,49152]{1,0:T(8,128)} reshape(f32[2,256,12,64]{3,2,1,0:T(8,128)} %copy.46) | data formatting | bytes 3145728 | tf_op jit(solution)/shard_map/reshape;reshape | solution.py:143
  79.0 3.7 %copy.49 = f32[2,256,12,64]{3,2,1,0:T(8,128)} copy(f32[2,256,12,64]{1,3,2,0:T(8,128)S(1)} %convolution_bitcast_fusion.1) | data formatting | bytes 3145728 | tf_op jit(solution)/shard_map/nhqk,nqhd->nkhd/transpose | solution.py:134
  82.8 4.5 %reshape_reshape.39 = f32[8,49152]{1,0:T(8,128)} reshape(f32[2,256,12,64]{3,2,1,0:T(8,128)} %copy.49) | data formatting | bytes 3145728 | tf_op jit(solution)/shard_map/reshape;reshape | solution.py:143
  87.3 3.4 %broadcast_select_fusion.1 = (f32[8,49152]{1,0:T(8,128)}, f32[8,49152]{1,0:T(8,128)}) fusion(f32[8,49152]{1,0:T(8,128)S(1)} %copy-done.6, pred[8]{0:T(512)(128)(4,1)S(1)} %get-tuple-element.142, f32[8,49152]{1,0:T(8,128)} %reshape_reshape.39), kind=kLoop, calls=%fused_computation.38 | loop fusion | flops 786432 | bytes 6291464 | tf_op jit(solution)/shard_map/jit(_where)/select_n | solution.py:144
  90.7 5.1 %scatter_custom_fusion.1 = f32[12,49152]{1,0:T(8,128)} fusion(s32[8]{0:T(128)} %fusion.33, f32[8,49152]{1,0:T(8,128)} %get-tuple-element.154, f32[]{:T(128)} %constant.347.clone.1), kind=kCustom, calls=%fused_computation.13 | custom fusion | flops 393216 | bytes 2359808 | tf_op jit(solution)/shard_map/scatter-add | solution.py:146
  95.7 2.0 convert.17
  98.3 4.9 %scatter_custom_fusion = f32[12,49152]{1,0:T(8,128)} fusion(s32[8]{0:T(128)} %fusion.33, f32[8,49152]{1,0:T(8,128)} %get-tuple-element.153, f32[]{:T(128)} %constant.347.clone.1), kind=kCustom, calls=%fused_computation.15 | custom fusion | flops 393216 | bytes 2359808 | tf_op jit(solution)/shard_map/scatter-add | solution.py:146
  103.2 2.0 convert.16
  110.1 1.9 reshape_reshape.35
  112.0 2.9 %fusion.19 = f32[768,768]{1,0:T(8,128)} fusion(bf16[128,768]{0,1:T(8,128)(2,1)} %reshape_reshape.35, bf16[16,8,768]{2,1,0:T(8,128)(2,1)} %param.32), kind=kOutput, calls=%fused_computation.71 | convolution fusion | flops 150994944 | bytes 2752512 | tf_op jit(solution)/shard_map/dot_general | solution.py:207
  114.9 10.2 %collective-permute-done.5 = bf16[2,8,24,768]{3,2,1,0:T(8,128)(2,1)} collective-permute-done((bf16[2,8,24,768]{3,2,1,0:T(8,128)(2,1)}, bf16[2,8,24,768]{3,2,1,0:T(8,128)(2,1)}, u32[]{:S(2)}, u32[]{:S(2)}) %collective-permute-start.5) | collective-permute-done | bytes 589856 | tf_op jit(solution)/shard_map/ppermute | solution.py:22
  125.1 10.0 %collective-permute-done.4 = bf16[2,8,24,768]{3,2,1,0:T(8,128)(2,1)} collective-permute-done((bf16[2,8,24,768]{3,2,1,0:T(8,128)(2,1)}, bf16[2,8,24,768]{3,2,1,0:T(8,128)(2,1)}, u32[]{:S(2)}, u32[]{:S(2)}) %collective-permute-start.4) | collective-permute-done | bytes 589856 | tf_op jit(solution)/shard_map/ppermute | solution.py:21
  135.1 2.8 %pad_maximum_fusion.4 = (bf16[2,48,8,768]{3,2,1,0:T(8,128)(2,1)}, bf16[2,48,8,768]{3,2,1,0:T(8,128)(2,1)}) fusion(bf16[2,8,24,768]{3,2,1,0:T(8,128)(2,1)} %collective-permute-done.5, bf16[2,8,24,768]{3,2,1,0:T(8,128)(2,1)} %collective-permute-done.4, bf16[1,32,24,768]{3,2,1,0:T(8,128)(2,1)S(1)} %bitcast.90, bf16[1,32,24,768]{3,2,1,0:T(8,128)(2,1)S(1)} %bitcast.100), kind=kLoop, calls=%fused_computation.29 | loop fusion | flops 9437184 | bytes 5898240 | tf_op jit(solution)/shard_map/slice | solution.py:19
  137.9 4.1 %collective-permute-start.7 = (bf16[2,48,8,768]{3,2,1,0:T(8,128)(2,1)}, bf16[2,48,8,768]{3,2,1,0:T(8,128)(2,1)}, u32[]{:S(2)}, u32[]{:S(2)}) collective-permute-start(bf16[2,48,8,768]{3,2,1,0:T(8,128)(2,1)} %get-tuple-element.144), channel_id=1, source_target_pairs={{1,0},{2,1},{3,2},{4,3},{5,4},{6,5},{7,6},{0,7},{9,8},{10,9},{11,1... | collective-permute-start | bytes 3538952 | tf_op jit(solution)/shard_map/ppermute | solution.py:22
  143.1 2.2 copy.44
  145.3 2.1 reshape_transpose_reshape_reshape.7
  147.4 2.0 fusion.10
  149.3 102.2 %all-reduce.2.cloned.1.call-done = f32[768,768]{1,0:T(8,128)} async-done(((f32[768,768]{1,0:T(8,128)}), f32[768,768]{1,0:T(8,128)}) %all-reduce.2.cloned.1.call-update) | async-done | bytes 2359312 | tf_op jit(solution)/shard_map/psum | solution.py:210
  251.6 3.2 %broadcast_multiply_fusion = f32[768,768]{1,0:T(8,128)} fusion(f32[768,768]{1,0:T(8,128)} %all-reduce.2.cloned.1.call-done), kind=kLoop, calls=%fused_computation.30 | loop fusion | flops 589824 | bytes 4718592 | tf_op jit(solution)/shard_map/div | solution.py:210
  (93 shorter events, 36.5 us)
Async XLA Ops:
  7.2 8.3 %copy-start = (bf16[768,768]{1,0:T(8,128)(2,1)S(1)}, bf16[768,768]{1,0:T(8,128)(2,1)}, u32[]{:S(2)}) copy-start(bf16[768,768]{1,0:T(8,128)(2,1)} %param.33) | copy-start | bytes 3538948
  7.2 14.6 %copy-start.9 = (bf16[16,8,768]{2,1,0:T(8,128)(2,1)S(1)}, bf16[16,8,768]{2,1,0:T(8,128)(2,1)}, u32[]{:S(2)}) copy-start(bf16[16,8,768]{2,1,0:T(8,128)(2,1)} %param.30) | copy-start | bytes 589828
  7.2 14.6 %copy-start.10 = (bf16[16,8,768]{2,1,0:T(8,128)(2,1)S(1)}, bf16[16,8,768]{2,1,0:T(8,128)(2,1)}, u32[]{:S(2)}) copy-start(bf16[16,8,768]{2,1,0:T(8,128)(2,1)} %param.31) | copy-start | bytes 589828
  7.2 244.4 %all-reduce.2.cloned.1.call-start = ((), (), s32[]{:S(2)}) async-start(), calls=%async_computation | async-start | bytes 4718592 | tf_op jit(solution)/shard_map/psum | solution.py:210
  8.4 9.3 %collective-permute-start.1 = (bf16[2,8,8,768]{3,2,1,0:T(8,128)(2,1)S(1)}, bf16[2,8,8,768]{3,2,1,0:T(8,128)(2,1)S(1)}, u32[]{:S(2)}, u32[]{:S(2)}) collective-permute-start(bf16[2,8,8,768]{3,2,1,0:T(8,128)(2,1)S(1)} %get-tuple-element.152), channel_id=1, source_target_pairs={{8,0},{16,8},{24,16},{0,24},{9,1},{17,9},{25,17},{1,25},{10,2},{18... | collective-permute-start | bytes 589832 | tf_op jit(solution)/shard_map/ppermute | solution.py:22
  12.4 9.4 %collective-permute-start = (bf16[2,8,8,768]{3,2,1,0:T(8,128)(2,1)S(1)}, bf16[2,8,8,768]{3,2,1,0:T(8,128)(2,1)S(1)}, u32[]{:S(2)}, u32[]{:S(2)}) collective-permute-start(bf16[2,8,8,768]{3,2,1,0:T(8,128)(2,1)S(1)} %get-tuple-element.151), channel_id=1, source_target_pairs={{0,8},{8,16},{16,24},{24,0},{1,9},{9,17},{17,25},{25,1},{2,10},{10... | collective-permute-start | bytes 589832 | tf_op jit(solution)/shard_map/ppermute | solution.py:21
  22.8 19.3 %collective-permute-start.3 = (bf16[2,32,8,768]{3,2,1,0:T(8,128)(2,1)}, bf16[2,32,8,768]{3,2,1,0:T(8,128)(2,1)S(1)}, u32[]{:S(2)}, u32[]{:S(2)}) collective-permute-start(bf16[2,32,8,768]{3,2,1,0:T(8,128)(2,1)} %pad_maximum_fusion.5), channel_id=1, source_target_pairs={{1,0},{2,1},{3,2},{4,3},{5,4},{6,5},{7,6},{0,7},{9,8},{10,9},{11,1... | collective-permute-start | bytes 2359304 | tf_op jit(solution)/shard_map/ppermute | solution.py:22
  24.9 20.1 %collective-permute-start.2 = (bf16[2,32,8,768]{3,2,1,0:T(8,128)(2,1)}, bf16[2,32,8,768]{3,2,1,0:T(8,128)(2,1)}, u32[]{:S(2)}, u32[]{:S(2)}) collective-permute-start(bf16[2,32,8,768]{3,2,1,0:T(8,128)(2,1)} %pad_maximum_fusion.5), channel_id=1, source_target_pairs={{0,1},{1,2},{2,3},{3,4},{4,5},{5,6},{6,7},{7,0},{8,9},{9,10},{10,1... | collective-permute-start | bytes 2359304 | tf_op jit(solution)/shard_map/ppermute | solution.py:21
  48.2 1.5 copy-start.8
  62.0 2.4 copy-start.5
  64.3 1.1 copy-start.3
  66.7 1.7 copy-start.7
  67.4 1.0 copy-start.1
  82.8 4.5 %copy-start.6 = (f32[8,49152]{1,0:T(8,128)S(1)}, f32[8,49152]{1,0:T(8,128)}, u32[]{:S(2)}) copy-start(f32[8,49152]{1,0:T(8,128)} %reshape_reshape.37) | copy-start | bytes 4718596
  105.7 3.2 %copy-start.11 = (bf16[2,64,12,64]{1,3,2,0:T(8,128)(2,1)S(1)}, bf16[2,64,12,64]{1,3,2,0:T(8,128)(2,1)}, u32[]{:S(2)}) copy-start(bf16[2,64,12,64]{1,3,2,0:T(8,128)(2,1)} %get-tuple-element.162) | copy-start | bytes 589828
  106.9 18.2 %collective-permute-start.5 = (bf16[2,8,24,768]{3,2,1,0:T(8,128)(2,1)}, bf16[2,8,24,768]{3,2,1,0:T(8,128)(2,1)}, u32[]{:S(2)}, u32[]{:S(2)}) collective-permute-start(bf16[2,8,24,768]{3,2,1,0:T(8,128)(2,1)} %get-tuple-element.146), channel_id=1, source_target_pairs={{8,0},{16,8},{24,16},{0,24},{9,1},{17,9},{25,17},{1,25},{10,2},{18... | collective-permute-start | bytes 1769480 | tf_op jit(solution)/shard_map/ppermute | solution.py:22
  108.3 26.7 %collective-permute-start.4 = (bf16[2,8,24,768]{3,2,1,0:T(8,128)(2,1)}, bf16[2,8,24,768]{3,2,1,0:T(8,128)(2,1)}, u32[]{:S(2)}, u32[]{:S(2)}) collective-permute-start(bf16[2,8,24,768]{3,2,1,0:T(8,128)(2,1)} %get-tuple-element.145), channel_id=1, source_target_pairs={{0,8},{8,16},{16,24},{24,0},{1,9},{9,17},{17,25},{25,1},{2,10},{10... | collective-permute-start | bytes 1769480 | tf_op jit(solution)/shard_map/ppermute | solution.py:21
  114.9 27.1 %copy-start.2 = (bf16[2,12,64,256]{3,2,1,0:T(8,128)(2,1)S(1)}, bf16[2,12,64,256]{3,2,1,0:T(8,128)(2,1)}, u32[]{:S(2)}) copy-start(bf16[2,12,64,256]{3,2,1,0:T(8,128)(2,1)} %copy-done.1) | copy-start | bytes 2359300
  114.9 27.1 %copy-start.4 = (bf16[2,256,12,64]{1,3,2,0:T(8,128)(2,1)S(1)}, bf16[2,256,12,64]{1,3,2,0:T(8,128)(2,1)}, u32[]{:S(2)}) copy-start(bf16[2,256,12,64]{1,3,2,0:T(8,128)(2,1)} %copy.35) | copy-start | bytes 2359300
  137.9 116.9 %collective-permute-start.7 = (bf16[2,48,8,768]{3,2,1,0:T(8,128)(2,1)}, bf16[2,48,8,768]{3,2,1,0:T(8,128)(2,1)}, u32[]{:S(2)}, u32[]{:S(2)}) collective-permute-start(bf16[2,48,8,768]{3,2,1,0:T(8,128)(2,1)} %get-tuple-element.144), channel_id=1, source_target_pairs={{1,0},{2,1},{3,2},{4,3},{5,4},{6,5},{7,6},{0,7},{9,8},{10,9},{11,1... | collective-permute-start | bytes 3538952 | tf_op jit(solution)/shard_map/ppermute | solution.py:22
  142.0 112.8 %collective-permute-start.6 = (bf16[2,48,8,768]{3,2,1,0:T(8,128)(2,1)}, bf16[2,48,8,768]{3,2,1,0:T(8,128)(2,1)}, u32[]{:S(2)}, u32[]{:S(2)}) collective-permute-start(bf16[2,48,8,768]{3,2,1,0:T(8,128)(2,1)} %get-tuple-element.143), channel_id=1, source_target_pairs={{0,1},{1,2},{2,3},{3,4},{4,5},{5,6},{6,7},{7,0},{8,9},{9,10},{10,1... | collective-permute-start | bytes 3538952 | tf_op jit(solution)/shard_map/ppermute | solution.py:21
Sparse Core Ops, SparseCore 0:
  115.0 136.5 all-reduce.1
where the time goes:
time: 271 us; the launch traced here: 270 us
  waiting for transfers between devices  142 us (52%)
  local copies, waits for them, and re-layouts  48.2 us (18%)
  other arithmetic  39.8 us (15%)
  between operations  14.4 us (5%)
  matrix products  13.1 us (5%)
  starting transfers between devices  12.4 us (5%)
    psum x1, waiting for transfers between devices, on_device(): w_grad = lax.psum(local_weight, ('lat', 'lon')) / math.sqrt(tokens_all)  102 us
    ppermute x4, waiting for transfers between devices, padded_2(): after = lax.ppermute(leading, axis, down)  23 us
    ppermute x4, waiting for transfers between devices, padded_2(): before = lax.ppermute(last, axis, up)  17.1 us
    another operation x8, local copies, waits for them, and re-layouts, split_heads(): block_tiles.reshape(block_tiles.shape[0], block_tiles.shape[1], HEADS, HE...  13.6 us
    ppermute x4, starting transfers between devices, padded_2(): after = lax.ppermute(leading, axis, down)  11.7 us
    scatter-add x2, other arithmetic, add_into(): jnp.zeros((pad_count, BLK * BLK * feat_width), jnp.float32).at[flat_place]  9.96 us
    another operation x2, local copies, waits for them, and re-layouts, add_into(): flat_terms = contrib.reshape(flat_place.shape[0], BLK * BLK * feat_width)  8.94 us
    transpose x2, local copies, waits for them, and re-layouts, contract_keys(): jnp.einsum('nhqk,nqhd->nkhd', weights_low, split_heads(block_tiles), pref...  8.46 us
  transfers between devices with their start and end apart: 9, of which 7 were waited for; matrix products, arithmetic and copies ran while one was open for 11% of the time, Pallas kernels for 0%

commit v1 on v0

v1 whole, which is shorter than its diff:
```python
import functools
import math

import jax
import jax.numpy as jnp
from jax import lax
from jax.experimental import pallas as pl
from jax.experimental.pallas import tpu as pltpu
from jax.sharding import PartitionSpec as P

HEAD_DIM = 64
BLK = 8
INNER = BLK * BLK
SLOTS = 4
PAIR = 2 * HEAD_DIM
NEG = -1e30
BOTH = ("lat", "lon")

VMEM = pl.BlockSpec(memory_space=pltpu.VMEM)
SMEM = pl.BlockSpec(memory_space=pltpu.SMEM)


def swap(pairs):
    return [(a, b) for a, b in pairs] + [(b, a) for a, b in pairs]


def slot_places(table, nb, lon_total):
    lat_index, lon_index = table[nb * SLOTS + nb], table[nb * SLOTS + nb + 1]
    even = lax.rem(lon_index, 2) == 0
    places = []
    for q in range(nb):
        row = []
        for s in range(SLOTS):
            block = table[q * SLOTS + s]
            lat_block = block // lon_total
            lon_block = block - lat_block * lon_total
            right = lon_block == lax.rem(lon_index + 1, lon_total)
            side = jnp.where(right == even, 1, 2)
            column = jnp.where(lon_block == lon_index, 0, side)
            row.append(column * (nb + 2) + lat_block - lat_index * nb + 1)
        places.append(row)
    return places


def edge_rows(table, nb):
    even = lax.rem(table[nb * SLOTS + nb], 2) == 0
    return jnp.where(even, nb + 1, 0), jnp.where(even, 0, nb + 1)


def fill(ext, table, nb, own, side_a, side_b, edge_e, edge_f, corner_a, corner_b):
    row_e, row_f = edge_rows(table, nb)
    step = nb + 2
    for kv in range(2):
        for r in range(nb):
            ext[kv, r + 1] = own[kv, r]
            ext[kv, step + r + 1] = side_a[kv, r]
            ext[kv, 2 * step + r + 1] = side_b[kv, r]
        for row, edge, index in ((row_e, edge_e, 0), (row_f, edge_f, 1)):
            ext[kv, row] = edge[kv]
            ext[kv, step + row] = corner_a[index, kv]
            ext[kv, 2 * step + row] = corner_b[index, kv]


def head_masks(value):
    low = lax.broadcasted_iota(jnp.int32, (INNER, PAIR), 1) < HEAD_DIM
    return (
        jnp.where(low, value, 0.0).astype(jnp.bfloat16),
        jnp.where(low, 0.0, value).astype(jnp.bfloat16),
        low,
    )


def two_heads(x, masks):
    return jnp.concatenate([x * masks[0], x * masks[1]], axis=0)


def dot(a, b, dims):
    return lax.dot_general(a, b, (dims, ((), ())), preferred_element_type=jnp.float32)


def probabilities(q2, keys, valid):
    scores = jnp.where(valid, dot(q2, keys, ((1,), (1,))), NEG)
    top = jnp.max(scores, axis=1, keepdims=True)
    weight = jnp.exp(scores - top)
    return weight / jnp.sum(weight, axis=1, keepdims=True)


def key_set(ext, kv, places, cols):
    return jnp.concatenate([ext[kv, place, :, cols] for place in places], axis=0)


def forward_kernel(nb, lon_total, table, q_ref, *refs):
    *inputs, att_ref, ext = refs
    fill(ext, table, nb, *inputs)
    places = slot_places(table, nb, lon_total)
    masks = head_masks(1.0 / math.sqrt(HEAD_DIM))
    low = masks[2]
    slot = lax.broadcasted_iota(jnp.int32, (2 * INNER, SLOTS * INNER), 1) // INNER
    for q in range(nb):
        valid = slot < table[nb * SLOTS + q]
        for p in range(q_ref.shape[-1] // PAIR):
            cols = slice(p * PAIR, (p + 1) * PAIR)
            q2 = two_heads(q_ref[q, :, cols], masks)
            probs = probabilities(q2, key_set(ext, 0, places[q], cols), valid)
            mixed = dot(
                probs.astype(jnp.bfloat16), key_set(ext, 1, places[q], cols), ((1,), (0,))
            )
            att_ref[q, :, cols] = jnp.where(low, mixed[:INNER], mixed[INNER:]).astype(
                jnp.bfloat16
            )


def backward_kernel(nb, lon_total, table, q_ref, da_ref, att_ref, *refs):
    *inputs, dq_ref, own_ref, edge_ref, a_ref, bc_ref, bo_ref, ext, acc = refs
    fill(ext, table, nb, *inputs)
    places = slot_places(table, nb, lon_total)
    scale = 1.0 / math.sqrt(HEAD_DIM)
    masks = head_masks(scale)
    ones = head_masks(1.0)
    low = masks[2]
    slot = lax.broadcasted_iota(jnp.int32, (2 * INNER, SLOTS * INNER), 1) // INNER
    acc[...] = jnp.zeros_like(acc)
    for q in range(nb):
        valid = slot < table[nb * SLOTS + q]
        for p in range(q_ref.shape[-1] // PAIR):
            cols = slice(p * PAIR, (p + 1) * PAIR)
            q2 = two_heads(q_ref[q, :, cols], masks)
            keys = key_set(ext, 0, places[q], cols)
            values = key_set(ext, 1, places[q], cols)
            probs = probabilities(q2, keys, valid)
            da = da_ref[q, :, cols]
            da2 = two_heads(da, ones)
            product = da.astype(jnp.float32) * att_ref[q, :, cols].astype(jnp.float32)
            delta = jnp.concatenate(
                [
                    jnp.sum(jnp.where(low, product, 0.0), axis=1, keepdims=True),
                    jnp.sum(jnp.where(low, 0.0, product), axis=1, keepdims=True),
                ],
                axis=0,
            )
            dprobs = dot(da2, values, ((1,), (1,)))
            dscores = (probs * (dprobs - delta)).astype(jnp.bfloat16)
            dq2 = dot(dscores, keys, ((1,), (0,)))
            dq_ref[q, :, cols] = (jnp.where(low, dq2[:INNER], dq2[INNER:]) * scale).astype(
                jnp.bfloat16
            )
            dk = dot(dscores, q2, ((0,), (0,)))
            dv = dot(probs.astype(jnp.bfloat16), da2, ((0,), (0,)))
            for s in range(SLOTS):
                rows = slice(s * INNER, (s + 1) * INNER)
                acc[0, places[q][s], :, cols] += dk[rows]
                acc[1, places[q][s], :, cols] += dv[rows]
    row_e, row_f = edge_rows(table, nb)
    step = nb + 2
    for kv in range(2):
        for r in range(nb):
            own_ref[kv, r] = acc[kv, r + 1]
            a_ref[kv, r] = acc[kv, step + r + 1].astype(jnp.bfloat16)
            bo_ref[kv, r] = acc[kv, 2 * step + r + 1].astype(jnp.bfloat16)
        for index, row in ((0, row_e), (1, row_f)):
            edge_ref[index, kv] = acc[kv, row]
            a_ref[kv, nb + index] = acc[kv, step + row].astype(jnp.bfloat16)
            bc_ref[index, kv] = acc[kv, 2 * step + row].astype(jnp.bfloat16)


def weight_kernel(bits, att_own, att_other, up_own, up_other, send_ref, keep_ref):
    half = att_own.shape[1] // 2
    cols = pl.ds(pl.multiple_of(bits[0] * half, half), half)
    total = dot(att_own[:, cols], up_own[...], ((0,), (0,)))
    total += dot(att_other[:, cols], up_other[...], ((0,), (0,)))
    rows = half // 2
    first = bits[1] == 0
    keep_ref[...] = jnp.where(first, total[:rows], total[rows:])
    send_ref[...] = jnp.where(first, total[rows:], total[:rows]).astype(jnp.bfloat16)


def flips(size):
    assert size & (size - 1) == 0
    return [1 << k for k in range(size.bit_length() - 1)]


def sum_over_mesh(att, upstream, up_other, att_other, lat_size, lon_size):
    lat_index, lon_index = lax.axis_index("lat"), lax.axis_index("lon")
    core = lon_index % 2
    lat_flips, lon_flips = flips(lat_size), flips(lon_size)[1:]
    lat_orders = (lat_flips, lat_flips[::-1])
    lon_orders = (lon_flips, lon_flips[::-1])

    def exchange(value, step, on_lat):
        pairs = []
        for a in range(lat_size):
            for o in range(lon_size):
                if on_lat:
                    to = (a ^ lat_orders[o % 2][step], o)
                else:
                    to = (a, o ^ lon_orders[o % 2][step])
                pairs.append((a * lon_size + o, to[0] * lon_size + to[1]))
        return lax.ppermute(value, BOTH, pairs)

    sides = [
        (lat_index // jnp.where(core == 0, one, two)) % 2 for one, two in zip(*lat_orders)
    ]
    width = att.shape[1]
    rows = width // 4
    send, total = pl.pallas_call(
        weight_kernel,
        out_shape=(
            jax.ShapeDtypeStruct((rows, width), jnp.bfloat16),
            jax.ShapeDtypeStruct((rows, width), jnp.float32),
        ),
        in_specs=[SMEM] + [VMEM] * 4,
        out_specs=(VMEM, VMEM),
        name="weight",
    )(jnp.stack([core, sides[0]]).astype(jnp.int32), att, att_other, upstream, up_other)
    total = total + exchange(send, 0, True).astype(jnp.float32)
    for step in range(1, len(lat_flips)):
        halves = total.reshape(2, -1, width)
        keep = lax.dynamic_index_in_dim(halves, sides[step], 0, keepdims=False)
        send = lax.dynamic_index_in_dim(halves, 1 - sides[step], 0, keepdims=False)
        got = exchange(send.astype(jnp.bfloat16), step, True)
        total = keep + got.astype(jnp.float32)
    low = total.astype(jnp.bfloat16)
    for step in range(len(lon_flips)):
        got = exchange(low, step, False)
        low = (low.astype(jnp.float32) + got.astype(jnp.float32)).astype(jnp.bfloat16)
    for step in reversed(range(len(lat_flips))):
        got = exchange(low, step, True)
        mine = lax.broadcasted_iota(jnp.int32, (2, 1, 1), 0) == sides[step]
        low = jnp.where(mine, low[None], got[None]).reshape(-1, width)
    other = lax.ppermute(low, "lon", swap([(o, o + 1) for o in range(0, lon_size, 2)]))
    mine = lax.broadcasted_iota(jnp.int32, (2, 1, 1), 0) == core
    return jnp.where(mine, low[None], other[None]).reshape(width, width).astype(jnp.float32)


def on_device(queries, key_vectors, value_vectors, upstream, w_out, neighbours, counts):
    lat_rows, lon_cols, width = queries.shape
    assert lon_cols == BLK
    nb = lat_rows // BLK
    lat_size, lon_size = lax.axis_size("lat"), lax.axis_size("lon")
    lat_index, lon_index = lax.axis_index("lat"), lax.axis_index("lon")
    lon_total = neighbours.shape[1]
    even = lat_index % 2 == 0
    pairs_a = swap([(o, o + 1) for o in range(0, lon_size, 2)])
    pairs_b = swap([(o, (o + 1) % lon_size) for o in range(1, lon_size, 2)])
    pairs_e = swap([(a, a + 1) for a in range(0, lat_size, 2)])
    pairs_f = swap([(a, a + 1) for a in range(1, lat_size - 1, 2)])

    blocks = (nb, INNER, width)
    kv = jnp.stack([key_vectors.reshape(blocks), value_vectors.reshape(blocks)])
    q_tiles = queries.reshape(blocks)
    edge = jnp.where(even, nb - 1, 0)

    side_b = lax.ppermute(kv, "lon", pairs_b)
    send_e = lax.dynamic_index_in_dim(kv, edge, 1, keepdims=False)
    send_f = lax.dynamic_index_in_dim(kv, nb - 1 - edge, 1, keepdims=False)
    edge_e = lax.ppermute(send_e, "lat", pairs_e)
    edge_f = lax.ppermute(send_f, "lat", pairs_f)
    side_a = lax.ppermute(kv, "lon", pairs_a)
    edges = jnp.stack([edge_e, edge_f])
    corner_b = lax.ppermute(edges, "lon", pairs_b)
    corner_a = lax.ppermute(edges, "lon", pairs_a)
    up_flat = upstream.reshape(-1, width)
    up_other = lax.ppermute(up_flat, "lon", pairs_a)

    slots = lax.dynamic_slice(neighbours, (lat_index * nb, lon_index, 0), (nb, 1, SLOTS))
    limits = lax.dynamic_slice(counts, (lat_index * nb, lon_index), (nb, 1))
    table = jnp.concatenate(
        [slots.reshape(-1), limits.reshape(-1), jnp.stack([lat_index, lon_index])]
    )
    d_att = dot(up_flat, w_out, ((1,), (1,))).astype(jnp.bfloat16)

    extended = (kv, side_a, side_b, edge_e, edge_f, corner_a, corner_b)
    ext = pltpu.VMEM((2, 3 * (nb + 2), INNER, width), jnp.bfloat16)
    att = pl.pallas_call(
        functools.partial(forward_kernel, nb, lon_total),
        out_shape=jax.ShapeDtypeStruct(blocks, jnp.bfloat16),
        in_specs=[SMEM] + [VMEM] * 8,
        out_specs=VMEM,
        scratch_shapes=[ext],
        name="forward",
    )(table, q_tiles, *extended)
    att_flat = att.reshape(-1, width)
    att_other = lax.ppermute(att_flat, "lon", pairs_a)
    w_sum = sum_over_mesh(att_flat, up_flat, up_other, att_other, lat_size, lon_size)
    tokens = lat_rows * lon_cols * lat_size * lon_size
    w_grad = w_sum * (1.0 / math.sqrt(tokens))

    low, full = jnp.bfloat16, jnp.float32
    q_grad, own, edge_sum, back_a, back_bc, back_bo = pl.pallas_call(
        functools.partial(backward_kernel, nb, lon_total),
        out_shape=(
            jax.ShapeDtypeStruct(blocks, low),
            jax.ShapeDtypeStruct((2,) + blocks, full),
            jax.ShapeDtypeStruct((2, 2, INNER, width), full),
            jax.ShapeDtypeStruct((2, nb + 2, INNER, width), low),
            jax.ShapeDtypeStruct((2, 2, INNER, width), low),
            jax.ShapeDtypeStruct((2,) + blocks, low),
        ),
        in_specs=[SMEM] + [VMEM] * 10,
        out_specs=(VMEM,) * 6,
        scratch_shapes=[ext, pltpu.VMEM((2, 3 * (nb + 2), INNER, width), full)],
        name="backward",
    )(table, q_tiles, d_att.reshape(blocks), att, *extended)
    mixed = dot(att_flat, w_out, ((1,), (0,))).astype(low)

    got_bc = lax.ppermute(back_bc, "lon", pairs_b)
    got_a = lax.ppermute(back_a, "lon", pairs_a)
    got_bo = lax.ppermute(back_bo, "lon", pairs_b)
    edge_sum = edge_sum + got_bc.astype(full)
    edge_sum = edge_sum + jnp.swapaxes(got_a[:, nb:], 0, 1).astype(full)
    edge_sum = edge_sum.astype(low)
    got_e = lax.ppermute(edge_sum[0], "lat", pairs_e)
    got_f = lax.ppermute(edge_sum[1], "lat", pairs_f)
    total = own + got_a[:, :nb].astype(full) + got_bo.astype(full)
    row = lax.broadcasted_iota(jnp.int32, (1, nb, 1, 1), 1)
    total = total + jnp.where(row == edge, got_e[:, None].astype(full), 0.0)
    total = total + jnp.where(row == nb - 1 - edge, got_f[:, None].astype(full), 0.0)
    total = total.astype(low)
    shape = queries.shape
    return (
        mixed.reshape(shape),
        q_grad.reshape(shape),
        total[0].reshape(shape),
        total[1].reshape(shape),
        w_grad,
    )


def solution(mesh):
    grid = P("lat", "lon", None)
    return jax.shard_map(
        on_device,
        mesh=mesh,
        in_specs=(grid, grid, grid, grid, P(), P(), P()),
        out_specs=(grid, grid, grid, grid, P()),
        check_vma=False,
    )
```

time: 271 us -> 105 us (0.39)
  waiting for transfers between devices: 142 us -> 37.1 us
  local copies, waits for them, and re-layouts: 48.2 us -> 8.23 us
  other arithmetic: 39.8 us -> 11.6 us
  Pallas kernels: 0 us -> 15.5 us
  starting transfers between devices: 12.4 us -> 27.5 us
  between operations: 14.4 us -> 0.89 us
  matrix products: 13.1 us -> 3.17 us
    psum x1 -> x0, waiting for transfers between devices: 102 us -> none  [on_device(): w_grad = lax.psum(local_weight, ('lat', 'lon')) / math.sqrt(tokens_all)]
    another operation x12 -> x0, local copies, waits for them, and re-layouts: 26.5 us -> none  [the longest x8 13.6 us: split_heads(): block_tiles.reshape(block_tiles.shape[0], block_tiles.shape[1], HEADS, HE...]
    scatter-add x8 -> x0, other arithmetic: 16.1 us -> none  [the longest x2 9.96 us: add_into(): jnp.zeros((pad_count, BLK * BLK * feat_width), jnp.float32).at[flat_place]]
    pallas_call x0 -> x3, Pallas kernels: none -> 15.5 us  [the longest x1 9.04 us: on_device(): pl.pallas_call(functools.partial(backward_kernel, nb, lon_total), out_sha...]
    ppermute x8 -> x20, starting transfers between devices: 12.3 us -> 27.5 us  [the longest x6 10 us: exchange(): return lax.ppermute(value, BOTH, pairs)]
    dot_general x9 -> x2, matrix products: 13.1 us -> 3.17 us  [dot(): lax.dot_general(a, b, (dims, ((), ())), preferred_element_type=jnp.float32)]
    transpose x6 -> x0, local copies, waits for them, and re-layouts: 8.85 us -> none  [the longest x2 8.46 us: contract_keys(): jnp.einsum('nhqk,nqhd->nkhd', weights_low, split_heads(block_tiles), pref...]
    select_n x7 -> x2, other arithmetic: 6.84 us -> 0.23 us  [sum_over_mesh(): low = jnp.where(mine, low[None], got[None]).reshape(-1, width)]
  transfers between devices with their start and end apart: 9 -> 20, of which waited for: 7 -> 9; matrix products, arithmetic and copies ran while one was open for 11% -> 17% of each run, Pallas kernels for 0% -> 12%
where the time goes in v1:
time: 105 us; the launch traced here: 104 us
  waiting for transfers between devices  37.1 us (35%)
  starting transfers between devices  27.5 us (26%)
  Pallas kernels  15.5 us (15%)
  other arithmetic  11.6 us (11%)
  local copies, waits for them, and re-layouts  8.23 us (8%)
  matrix products  3.17 us (3%)
    ppermute x6, waiting for transfers between devices, exchange(): return lax.ppermute(value, BOTH, pairs)  22.6 us
    ppermute x6, starting transfers between devices, exchange(): return lax.ppermute(value, BOTH, pairs)  10 us
    pallas_call x1, Pallas kernels, on_device(): pl.pallas_call(functools.partial(backward_kernel, nb, lon_total), out_sha...  9.04 us
    ppermute x1, waiting for transfers between devices, on_device(): corner_b = lax.ppermute(edges, 'lon', pairs_b)  7.84 us
    pallas_call x1, Pallas kernels, on_device(): pl.pallas_call(functools.partial(forward_kernel, nb, lon_total), out_shap...  3.84 us
    ppermute x1, starting transfers between devices, on_device(): side_b = lax.ppermute(kv, 'lon', pairs_b)  3.7 us
    ppermute x1, starting transfers between devices, on_device(): corner_b = lax.ppermute(edges, 'lon', pairs_b)  3.47 us
    dot_general x2, matrix products, dot(): lax.dot_general(a, b, (dims, ((), ())), preferred_element_type=jnp.float32)  3.17 us
  transfers between devices with their start and end apart: 20, of which 9 were waited for; matrix products, arithmetic and copies ran while one was open for 17% of the time, Pallas kernels for 12%

profile of v1, /device:TPU:0, one launch (start us, length us, event | category | flops | bytes accessed | tf_op | source)
XLA Modules:
  0.0 104.0 jit_solution(3281227238115319029)
XLA Ops:
  0.7 1.2 %fusion.6 = (bf16[2,64,768]{2,1,0:T(8,128)(2,1)S(1)}, bf16[2,64,768]{2,1,0:T(8,128)(2,1)S(1)}) fusion(s32[]{:T(128)S(6)} %select_n.90, bf16[1,2,64,768]{3,2,1,0:T(8,128)(2,1)} %bitcast.67, bf16[1,2,64,768]{3,2,1,0:T(8,128)(2,1)} %bitcast.65, s32[]{:T(128)S(6)} %select_n.89), kind=kLoop, calls=%fused_computation.26 | loop fusion | flops 196608 | bytes 786440 | tf_op jit(solution)/shard_map/jit(dynamic_index_in_dim)/squeeze | solution.py:255
  1.8 3.0 %collective-permute-start.2 = (bf16[2,64,768]{2,1,0:T(8,128)(2,1)S(1)}, bf16[2,64,768]{2,1,0:T(8,128)(2,1)S(1)}, u32[]{:S(2)}, u32[]{:S(2)}) collective-permute-start(bf16[2,64,768]{2,1,0:T(8,128)(2,1)S(1)} %get-tuple-element.26), channel_id=1, source_target_pairs={{0,8},{16,24},{8,0},{24,16},{1,9},{17,25},{9,1},{25,17},{2,10},{18... | collective-permute-start | bytes 589832 | tf_op jit(solution)/shard_map/ppermute | solution.py:256
  5.5 1.1 %pad_maximum_fusion.refs_0_ = bf16[2,2,64,768]{3,2,1,0:T(8,128)(2,1)S(1)} fusion(bf16[1,2,64,768]{3,2,1,0:T(8,128)(2,1)} %bitcast.66, bf16[1,2,64,768]{3,2,1,0:T(8,128)(2,1)} %bitcast.68), kind=kLoop, calls=%fused_computation.13 | loop fusion | flops 196608 | bytes 786432 | tf_op jit(solution)/shard_map/stack | solution.py:249
  6.7 3.7 %collective-permute-start.1 = (bf16[2,2,64,768]{3,2,1,0:T(8,128)(2,1)S(1)}, bf16[2,2,64,768]{3,2,1,0:T(8,128)(2,1)S(1)}, u32[]{:S(2)}, u32[]{:S(2)}) collective-permute-start(bf16[2,2,64,768]{3,2,1,0:T(8,128)(2,1)S(1)} %pad_maximum_fusion.refs_0_), channel_id=1, source_target_pairs={{1,2},{3,4},{5,6},{7,0},{2,1},{4,3},{6,5},{0,7},{9,10},{11,12},{13... | collective-permute-start | bytes 1179656 | tf_op jit(solution)/shard_map/ppermute | solution.py:253
  11.3 3.5 %collective-permute-start.5 = (bf16[2,2,64,768]{3,2,1,0:T(8,128)(2,1)}, bf16[2,2,64,768]{3,2,1,0:T(8,128)(2,1)S(1)}, u32[]{:S(2)}, u32[]{:S(2)}) collective-permute-start(bf16[2,2,64,768]{3,2,1,0:T(8,128)(2,1)} %pad_maximum_fusion.1), channel_id=1, source_target_pairs={{1,2},{3,4},{5,6},{7,0},{2,1},{4,3},{6,5},{0,7},{9,10},{11,12},{13... | collective-permute-start | bytes 1179656 | tf_op jit(solution)/shard_map/ppermute | solution.py:260
  15.6 0.9 dynamic-slice_reduce_fusion
  17.2 2.7 %collective-permute-done.1.refs_2_ = bf16[2,2,64,768]{3,2,1,0:T(8,128)(2,1)S(1)} collective-permute-done((bf16[2,2,64,768]{3,2,1,0:T(8,128)(2,1)S(1)}, bf16[2,2,64,768]{3,2,1,0:T(8,128)(2,1)S(1)}, u32[]{:S(2)}, u32[]{:S(2)}) %collective-permute-start.1) | collective-permute-done | bytes 393248 | tf_op jit(solution)/shard_map/ppermute | solution.py:253
  19.9 7.8 %collective-permute-done.5.refs_6_ = bf16[2,2,64,768]{3,2,1,0:T(8,128)(2,1)S(1)} collective-permute-done((bf16[2,2,64,768]{3,2,1,0:T(8,128)(2,1)}, bf16[2,2,64,768]{3,2,1,0:T(8,128)(2,1)S(1)}, u32[]{:S(2)}, u32[]{:S(2)}) %collective-permute-start.5) | collective-permute-done | bytes 393248 | tf_op jit(solution)/shard_map/ppermute | solution.py:260
  28.5 3.8 %forward.1.att_ref = bf16[2,64,768]{2,1,0:T(8,128)(2,1)} custom-call(s32[12]{0:T(128)} %pad_add_fusion.table, bf16[2,64,768]{2,1,0:T(8,128)(2,1)} %bitcast.62, bf16[2,2,64,768]{3,2,1,0:T(8,128)(2,1)} %copy-done.1, bf16[2,2,64,768]{3,2,1,0:T(8,128)(2,1)} %copy-done.5, bf16[2,2,64,768]{3,2,1,0:T(8,128)(2,1)} %copy-done.6, bf16[2,64,768]{2,1,0:T(8,128)(2,1)} %copy-done.3, ...), custom_call_target="tpu_custom_call" | custom-call | tf_op jit(solution)/shard_map/forward/pallas_call | solution.py:274
  33.0 1.0 collective-permute-done.11.att_other
  34.7 2.6 %weight.1 = (bf16[192,768]{1,0:T(8,128)(2,1)}, f32[192,768]{1,0:T(8,128)}) custom-call(s32[2]{0:T(128)} %pad_add_fusion.1.bits, bf16[128,768]{1,0:T(8,128)(2,1)} %bitcast.56, bf16[128,768]{1,0:T(8,128)(2,1)} %copy-done.11, bf16[128,768]{1,0:T(8,128)(2,1)} %bitcast.11.up_own, bf16[128,768]{1,0:T(8,128)(2,1)} %collective-permute-done.12.up_other), custom_call_target="tpu_custom_call" | custom-call | tf_op jit(solution)/shard_map/weight/pallas_call | solution.py:205
  37.3 4.2 %collective-permute-start.13 = (bf16[192,768]{1,0:T(8,128)(2,1)}, bf16[192,768]{1,0:T(8,128)(2,1)S(1)}, u32[]{:S(2)}, u32[]{:S(2)}) collective-permute-start(bf16[192,768]{1,0:T(8,128)(2,1)} %get-tuple-element.20), channel_id=1, source_target_pairs={{0,8},{1,17},{2,10},{3,19},{4,12},{5,21},{6,14},{7,23},{8,0},{9,25... | collective-permute-start | bytes 884744 | tf_op jit(solution)/shard_map/ppermute | solution.py:198
  41.5 4.9 %collective-permute-done.13 = bf16[192,768]{1,0:T(8,128)(2,1)S(1)} collective-permute-done((bf16[192,768]{1,0:T(8,128)(2,1)}, bf16[192,768]{1,0:T(8,128)(2,1)S(1)}, u32[]{:S(2)}, u32[]{:S(2)}) %collective-permute-start.13) | collective-permute-done | bytes 294944 | tf_op jit(solution)/shard_map/ppermute | solution.py:198
  46.4 1.1 %convert_add_fusion = f32[192,768]{1,0:T(8,128)S(1)} fusion(f32[192,768]{1,0:T(8,128)} %get-tuple-element.19, bf16[192,768]{1,0:T(8,128)(2,1)S(1)} %collective-permute-done.13), kind=kLoop, calls=%fused_computation.10 | loop fusion | flops 294912 | bytes 1474560 | tf_op jit(solution)/shard_map/add | solution.py:215
  47.6 1.1 %collective-permute-start.14 = (bf16[96,768]{1,0:T(8,128)(2,1)S(1)}, bf16[96,768]{1,0:T(8,128)(2,1)S(1)}, u32[]{:S(2)}, u32[]{:S(2)}) collective-permute-start(bf16[96,768]{1,0:T(8,128)(2,1)S(1)} %fusion.7), channel_id=1, source_target_pairs={{0,16},{1,9},{2,18},{3,11},{4,20},{5,13},{6,22},{7,15},{8,24},{9,1... | collective-permute-start | bytes 442376 | tf_op jit(solution)/shard_map/ppermute | solution.py:198
  48.7 2.2 %convolution_convert_fusion = bf16[128,768]{1,0:T(8,128)(2,1)} fusion(bf16[768,768]{1,0:T(8,128)(2,1)S(1)} %copy-done, bf16[16,8,768]{2,1,0:T(8,128)(2,1)} %param.10), kind=kOutput, calls=%fused_computation.2 | convolution fusion | flops 151093248 | bytes 1572864 | tf_op jit(solution)/shard_map/dot_general | solution.py:78
  50.8 1.9 %collective-permute-done.14 = bf16[96,768]{1,0:T(8,128)(2,1)S(1)} collective-permute-done((bf16[96,768]{1,0:T(8,128)(2,1)S(1)}, bf16[96,768]{1,0:T(8,128)(2,1)S(1)}, u32[]{:S(2)}, u32[]{:S(2)}) %collective-permute-start.14) | collective-permute-done | bytes 147488 | tf_op jit(solution)/shard_map/ppermute | solution.py:198
  53.4 9.0 %backward.1 = (bf16[2,64,768]{2,1,0:T(8,128)(2,1)}, f32[2,2,64,768]{3,2,1,0:T(8,128)}, f32[2,2,64,768]{3,2,1,0:T(8,128)}, bf16[2,4,64,768]{3,2,1,0:T(8,128)(2,1)...) custom-call(s32[12]{0:T(128)} %pad_add_fusion.table, bf16[2,64,768]{2,1,0:T(8,128)(2,1)} %bitcast.63, ...), custom_call_target="tpu_custom_call" | custom-call | tf_op jit(solution)/shard_map/backward/pallas_call | solution.py:289
  62.5 1.8 %copy.14 = bf16[2,2,64,768]{3,2,0,1:T(8,128)(2,1)} copy(bf16[2,2,64,768]{3,2,1,0:T(8,128)(2,1)} %get-tuple-element.18) | data formatting | bytes 786432 | tf_op jit(solution)/shard_map/backward/pallas_call | solution.py:289
  64.3 2.5 %collective-permute-start.8 = (bf16[2,2,64,768]{3,2,0,1:T(8,128)(2,1)}, bf16[2,2,64,768]{3,2,0,1:T(8,128)(2,1)S(1)}, u32[]{:S(2)}, u32[]{:S(2)}) collective-permute-start(bf16[2,2,64,768]{3,2,0,1:T(8,128)(2,1)} %copy.14), channel_id=1, source_target_pairs={{1,2},{3,4},{5,6},{7,0},{2,1},{4,3},{6,5},{0,7},{9,10},{11,12},{13... | collective-permute-start | bytes 1179656 | tf_op jit(solution)/shard_map/ppermute | solution.py:306
  66.7 1.0 add_convert_fusion.2
  69.4 10.4 %collective-permute-done.16 = bf16[96,768]{1,0:T(8,128)(2,1)} collective-permute-done((bf16[96,768]{1,0:T(8,128)(2,1)S(1)}, bf16[96,768]{1,0:T(8,128)(2,1)}, u32[]{:S(2)}, u32[]{:S(2)}) %collective-permute-start.16) | collective-permute-done | bytes 147488 | tf_op jit(solution)/shard_map/ppermute | solution.py:198
  79.8 1.0 add_convert_fusion.1
  80.8 1.1 %collective-permute-start.17 = (bf16[96,768]{1,0:T(8,128)(2,1)S(1)}, bf16[96,768]{1,0:T(8,128)(2,1)S(1)}, u32[]{:S(2)}, u32[]{:S(2)}) collective-permute-start(bf16[96,768]{1,0:T(8,128)(2,1)S(1)} %add_convert_fusion.1), channel_id=1, source_target_pairs={{0,16},{1,9},{2,18},{3,11},{4,20},{5,13},{6,22},{7,15},{8,24},{9,1... | collective-permute-start | bytes 442376 | tf_op jit(solution)/shard_map/ppermute | solution.py:198
  82.1 4.7 %collective-permute-done.17 = bf16[96,768]{1,0:T(8,128)(2,1)S(1)} collective-permute-done((bf16[96,768]{1,0:T(8,128)(2,1)S(1)}, bf16[96,768]{1,0:T(8,128)(2,1)S(1)}, u32[]{:S(2)}, u32[]{:S(2)}) %collective-permute-start.17) | collective-permute-done | bytes 147488 | tf_op jit(solution)/shard_map/ppermute | solution.py:198
  86.9 2.4 %collective-permute-start.18 = (bf16[192,768]{1,0:T(8,128)(2,1)S(1)}, bf16[192,768]{1,0:T(8,128)(2,1)S(1)}, u32[]{:S(2)}, u32[]{:S(2)}) collective-permute-start(bf16[192,768]{1,0:T(8,128)(2,1)S(1)} %bitcast_select_fusion.2), channel_id=1, source_target_pairs={{0,8},{1,17},{2,10},{3,19},{4,12},{5,21},{6,14},{7,23},{8,0},{9,25... | collective-permute-start | bytes 884744 | tf_op jit(solution)/shard_map/ppermute | solution.py:198
  90.0 2.5 %collective-permute-start.9 = (bf16[2,64,768]{2,1,0:T(8,128)(2,1)S(1)}, bf16[2,64,768]{2,1,0:T(8,128)(2,1)S(1)}, u32[]{:S(2)}, u32[]{:S(2)}) collective-permute-start(bf16[2,64,768]{2,1,0:T(8,128)(2,1)S(1)} %get-tuple-element.23), channel_id=1, source_target_pairs={{0,8},{16,24},{8,0},{24,16},{1,9},{17,25},{9,1},{25,17},{2,10},{18... | collective-permute-start | bytes 589832 | tf_op jit(solution)/shard_map/ppermute | solution.py:312
  93.1 1.3 %broadcast_in_dim.141 = pred[2,192]{1,0:T(4,128)(4,1)} broadcast(pred[2]{0:T(512)(128)(4,1)} %iota_compare_fusion.1), dimensions={0} | broadcast | bytes 386 | tf_op jit(solution)/shard_map/jit(_where)/broadcast_in_dim | solution.py:229
  96.0 1.0 fusion
  97.1 2.9 %collective-permute-done.9 = bf16[2,64,768]{2,1,0:T(8,128)(2,1)S(1)} collective-permute-done((bf16[2,64,768]{2,1,0:T(8,128)(2,1)S(1)}, bf16[2,64,768]{2,1,0:T(8,128)(2,1)S(1)}, u32[]{:S(2)}, u32[]{:S(2)}) %collective-permute-start.9) | collective-permute-done | bytes 196640 | tf_op jit(solution)/shard_map/ppermute | solution.py:312
  100.0 1.3 %add_convert_fusion = bf16[2,2,64,768]{3,2,1,0:T(8,128)(2,1)S(1)} fusion(bf16[2,2,64,768]{3,2,1,0:T(8,128)(2,1)} %collective-permute-done.7, f32[2,2,64,768]{3,2,1,0:T(8,128)S(1)} %copy-done.9, bf16[2,4,64,768]{3,2,1,0:T(8,128)(2,1)S(1)} %collective-permute-done.6, f32[2,64,768]{2,1,0:T(8,128)S(1)} %convert_element_type.80, ...), kind=kLoop, calls=%fused_computation.8 | loop fusion | flops 1769472 | bytes 2752516 | tf_op jit(solution)/shard_map/convert_element_type | solution.py:318
  102.1 1.9 %convert_multiply_fusion = f32[768,768]{1,0:T(8,128)} fusion(pred[768]{0:T(1024)(128)(4,1)S(1)} %broadcast_in_dim.139, bf16[384,768]{1,0:T(8,128)(2,1)S(1)} %collective-permute-done.19, bf16[384,768]{1,0:T(8,128)(2,1)S(1)} %bitcast_select_fusion.1), kind=kLoop, calls=%fused_computation | loop fusion | flops 1769472 | bytes 3539712 | tf_op jit(solution)/shard_map/mul | solution.py:286
  (71 shorter events, 11.6 us)
Async XLA Ops:
  0.6 48.0 %copy-start = (bf16[768,768]{1,0:T(8,128)(2,1)S(1)}, bf16[768,768]{1,0:T(8,128)(2,1)}, u32[]{:S(2)}) copy-start(bf16[768,768]{1,0:T(8,128)(2,1)} %param.11) | copy-start | bytes 3538948
  1.8 8.6 %collective-permute-start.2 = (bf16[2,64,768]{2,1,0:T(8,128)(2,1)S(1)}, bf16[2,64,768]{2,1,0:T(8,128)(2,1)S(1)}, u32[]{:S(2)}, u32[]{:S(2)}) collective-permute-start(bf16[2,64,768]{2,1,0:T(8,128)(2,1)S(1)} %get-tuple-element.26), channel_id=1, source_target_pairs={{0,8},{16,24},{8,0},{24,16},{1,9},{17,25},{9,1},{25,17},{2,10},{18... | collective-permute-start | bytes 589832 | tf_op jit(solution)/shard_map/ppermute | solution.py:256
  4.9 5.5 %collective-permute-start.3 = (bf16[2,64,768]{2,1,0:T(8,128)(2,1)S(1)}, bf16[2,64,768]{2,1,0:T(8,128)(2,1)S(1)}, u32[]{:S(2)}, u32[]{:S(2)}) collective-permute-start(bf16[2,64,768]{2,1,0:T(8,128)(2,1)S(1)} %get-tuple-element.25), channel_id=1, source_target_pairs={{8,16},{16,8},{9,17},{17,9},{10,18},{18,10},{11,19},{19,11},{12,20... | collective-permute-start | bytes 589832 | tf_op jit(solution)/shard_map/ppermute | solution.py:257
  6.6 21.2 %copy-start.1 = (bf16[2,2,64,768]{3,2,1,0:T(8,128)(2,1)}, bf16[2,2,64,768]{3,2,1,0:T(8,128)(2,1)S(1)}, u32[]{:S(2)}) copy-start(bf16[2,2,64,768]{3,2,1,0:T(8,128)(2,1)S(1)} %pad_maximum_fusion.refs_0_) | copy-start | bytes 1179652
  6.6 10.6 %collective-permute-start = (bf16[2,2,64,768]{3,2,1,0:T(8,128)(2,1)S(1)}, bf16[2,2,64,768]{3,2,1,0:T(8,128)(2,1)S(1)}, u32[]{:S(2)}, u32[]{:S(2)}) collective-permute-start(bf16[2,2,64,768]{3,2,1,0:T(8,128)(2,1)S(1)} %pad_maximum_fusion.refs_0_), channel_id=1, source_target_pairs={{0,1},{2,3},{4,5},{6,7},{1,0},{3,2},{5,4},{7,6},{8,9},{10,11},{12,... | collective-permute-start | bytes 1179656 | tf_op jit(solution)/shard_map/ppermute | solution.py:258
  6.7 13.2 %collective-permute-start.1 = (bf16[2,2,64,768]{3,2,1,0:T(8,128)(2,1)S(1)}, bf16[2,2,64,768]{3,2,1,0:T(8,128)(2,1)S(1)}, u32[]{:S(2)}, u32[]{:S(2)}) collective-permute-start(bf16[2,2,64,768]{3,2,1,0:T(8,128)(2,1)S(1)} %pad_maximum_fusion.refs_0_), channel_id=1, source_target_pairs={{1,2},{3,4},{5,6},{7,0},{2,1},{4,3},{6,5},{0,7},{9,10},{11,12},{13... | collective-permute-start | bytes 1179656 | tf_op jit(solution)/shard_map/ppermute | solution.py:253
  10.4 17.4 %copy-start.3 = (bf16[2,64,768]{2,1,0:T(8,128)(2,1)}, bf16[2,64,768]{2,1,0:T(8,128)(2,1)S(1)}, u32[]{:S(2)}) copy-start(bf16[2,64,768]{2,1,0:T(8,128)(2,1)S(1)} %collective-permute-done.2.refs_3_) | copy-start | bytes 589828
  10.4 17.4 %copy-start.4 = (bf16[2,64,768]{2,1,0:T(8,128)(2,1)}, bf16[2,64,768]{2,1,0:T(8,128)(2,1)S(1)}, u32[]{:S(2)}) copy-start(bf16[2,64,768]{2,1,0:T(8,128)(2,1)S(1)} %collective-permute-done.3.refs_4_) | copy-start | bytes 589828
  11.3 8.6 %collective-permute-start.4 = (bf16[2,2,64,768]{3,2,1,0:T(8,128)(2,1)}, bf16[2,2,64,768]{3,2,1,0:T(8,128)(2,1)S(1)}, u32[]{:S(2)}, u32[]{:S(2)}) collective-permute-start(bf16[2,2,64,768]{3,2,1,0:T(8,128)(2,1)} %pad_maximum_fusion.1), channel_id=1, source_target_pairs={{0,1},{2,3},{4,5},{6,7},{1,0},{3,2},{5,4},{7,6},{8,9},{10,11},{12,... | collective-permute-start | bytes 1179656 | tf_op jit(solution)/shard_map/ppermute | solution.py:261
  11.3 16.5 %collective-permute-start.5 = (bf16[2,2,64,768]{3,2,1,0:T(8,128)(2,1)}, bf16[2,2,64,768]{3,2,1,0:T(8,128)(2,1)S(1)}, u32[]{:S(2)}, u32[]{:S(2)}) collective-permute-start(bf16[2,2,64,768]{3,2,1,0:T(8,128)(2,1)} %pad_maximum_fusion.1), channel_id=1, source_target_pairs={{1,2},{3,4},{5,6},{7,0},{2,1},{4,3},{6,5},{0,7},{9,10},{11,12},{13... | collective-permute-start | bytes 1179656 | tf_op jit(solution)/shard_map/ppermute | solution.py:260
  14.7 18.3 %collective-permute-start.12 = (bf16[128,768]{1,0:T(8,128)(2,1)}, bf16[128,768]{1,0:T(8,128)(2,1)}, u32[]{:S(2)}, u32[]{:S(2)}) collective-permute-start(bf16[128,768]{1,0:T(8,128)(2,1)} %bitcast.11.up_own), channel_id=1, source_target_pairs={{0,1},{2,3},{4,5},{6,7},{1,0},{3,2},{5,4},{7,6},{8,9},{10,11},{12,... | collective-permute-start | bytes 589832 | tf_op jit(solution)/shard_map/ppermute | solution.py:263
  17.2 10.5 %copy-start.5 = (bf16[2,2,64,768]{3,2,1,0:T(8,128)(2,1)}, bf16[2,2,64,768]{3,2,1,0:T(8,128)(2,1)S(1)}, u32[]{:S(2)}) copy-start(bf16[2,2,64,768]{3,2,1,0:T(8,128)(2,1)S(1)} %collective-permute-done.refs_1_) | copy-start | bytes 1179652
  19.9 7.9 %copy-start.6 = (bf16[2,2,64,768]{3,2,1,0:T(8,128)(2,1)}, bf16[2,2,64,768]{3,2,1,0:T(8,128)(2,1)S(1)}, u32[]{:S(2)}) copy-start(bf16[2,2,64,768]{3,2,1,0:T(8,128)(2,1)S(1)} %collective-permute-done.1.refs_2_) | copy-start | bytes 1179652
  19.9 7.9 %copy-start.7 = (bf16[2,2,64,768]{3,2,1,0:T(8,128)(2,1)}, bf16[2,2,64,768]{3,2,1,0:T(8,128)(2,1)S(1)}, u32[]{:S(2)}) copy-start(bf16[2,2,64,768]{3,2,1,0:T(8,128)(2,1)S(1)} %collective-permute-done.4.refs_5_) | copy-start | bytes 1179652
  27.7 0.7 copy-start.8
  32.3 1.7 %collective-permute-start.11 = (bf16[128,768]{1,0:T(8,128)(2,1)}, bf16[128,768]{1,0:T(8,128)(2,1)S(1)}, u32[]{:S(2)}, u32[]{:S(2)}) collective-permute-start(bf16[128,768]{1,0:T(8,128)(2,1)} %bitcast.55), channel_id=1, source_target_pairs={{0,1},{2,3},{4,5},{6,7},{1,0},{3,2},{5,4},{7,6},{8,9},{10,11},{12,... | collective-permute-start | bytes 589832 | tf_op jit(solution)/shard_map/ppermute | solution.py:283
  34.0 0.7 copy-start.11
  37.3 9.1 %collective-permute-start.13 = (bf16[192,768]{1,0:T(8,128)(2,1)}, bf16[192,768]{1,0:T(8,128)(2,1)S(1)}, u32[]{:S(2)}, u32[]{:S(2)}) collective-permute-start(bf16[192,768]{1,0:T(8,128)(2,1)} %get-tuple-element.20), channel_id=1, source_target_pairs={{0,8},{1,17},{2,10},{3,19},{4,12},{5,21},{6,14},{7,23},{8,0},{9,25... | collective-permute-start | bytes 884744 | tf_op jit(solution)/shard_map/ppermute | solution.py:198
  47.6 5.2 %collective-permute-start.14 = (bf16[96,768]{1,0:T(8,128)(2,1)S(1)}, bf16[96,768]{1,0:T(8,128)(2,1)S(1)}, u32[]{:S(2)}, u32[]{:S(2)}) collective-permute-start(bf16[96,768]{1,0:T(8,128)(2,1)S(1)} %fusion.7), channel_id=1, source_target_pairs={{0,16},{1,9},{2,18},{3,11},{4,20},{5,13},{6,22},{7,15},{8,24},{9,1... | collective-permute-start | bytes 442376 | tf_op jit(solution)/shard_map/ppermute | solution.py:198
  52.8 13.9 %collective-permute-start.15 = (bf16[96,768]{1,0:T(8,128)(2,1)S(1)}, bf16[96,768]{1,0:T(8,128)(2,1)}, u32[]{:S(2)}, u32[]{:S(2)}) collective-permute-start(bf16[96,768]{1,0:T(8,128)(2,1)S(1)} %fusion.2), channel_id=1, source_target_pairs={{0,2},{1,5},{2,0},{3,7},{4,6},{5,1},{6,4},{7,3},{8,10},{9,13},{10,... | collective-permute-start | bytes 442376 | tf_op jit(solution)/shard_map/ppermute | solution.py:198
  62.4 19.5 %copy-start.10 = (f32[2,2,64,768]{3,2,1,0:T(8,128)S(1)}, f32[2,2,64,768]{3,2,1,0:T(8,128)}, u32[]{:S(2)}) copy-start(f32[2,2,64,768]{3,2,1,0:T(8,128)} %get-tuple-element.17) | copy-start | bytes 2359300
  62.4 19.5 %collective-permute-start.6 = (bf16[2,4,64,768]{3,2,1,0:T(8,128)(2,1)}, bf16[2,4,64,768]{3,2,1,0:T(8,128)(2,1)S(1)}, u32[]{:S(2)}, u32[]{:S(2)}) collective-permute-start(bf16[2,4,64,768]{3,2,1,0:T(8,128)(2,1)} %get-tuple-element.15), channel_id=1, source_target_pairs={{0,1},{2,3},{4,5},{6,7},{1,0},{3,2},{5,4},{7,6},{8,9},{10,11},{12,... | collective-permute-start | bytes 2359304 | tf_op jit(solution)/shard_map/ppermute | solution.py:307
  64.3 17.6 %collective-permute-start.8 = (bf16[2,2,64,768]{3,2,0,1:T(8,128)(2,1)}, bf16[2,2,64,768]{3,2,0,1:T(8,128)(2,1)S(1)}, u32[]{:S(2)}, u32[]{:S(2)}) collective-permute-start(bf16[2,2,64,768]{3,2,0,1:T(8,128)(2,1)} %copy.14), channel_id=1, source_target_pairs={{1,2},{3,4},{5,6},{7,0},{2,1},{4,3},{6,5},{0,7},{9,10},{11,12},{13... | collective-permute-start | bytes 1179656 | tf_op jit(solution)/shard_map/ppermute | solution.py:306
  67.7 12.1 %collective-permute-start.16 = (bf16[96,768]{1,0:T(8,128)(2,1)S(1)}, bf16[96,768]{1,0:T(8,128)(2,1)}, u32[]{:S(2)}, u32[]{:S(2)}) collective-permute-start(bf16[96,768]{1,0:T(8,128)(2,1)S(1)} %add_convert_fusion.2), channel_id=1, source_target_pairs={{0,4},{1,3},{2,6},{3,1},{4,0},{5,7},{6,2},{7,5},{8,12},{9,11},{10,... | collective-permute-start | bytes 442376 | tf_op jit(solution)/shard_map/ppermute | solution.py:198
  68.5 31.5 %collective-permute-start.7 = (bf16[2,2,64,768]{3,2,1,0:T(8,128)(2,1)}, bf16[2,2,64,768]{3,2,1,0:T(8,128)(2,1)}, u32[]{:S(2)}, u32[]{:S(2)}) collective-permute-start(bf16[2,2,64,768]{3,2,1,0:T(8,128)(2,1)} %get-tuple-element.16), channel_id=1, source_target_pairs={{1,2},{3,4},{5,6},{7,0},{2,1},{4,3},{6,5},{0,7},{9,10},{11,12},{13... | collective-permute-start | bytes 1179656 | tf_op jit(solution)/shard_map/ppermute | solution.py:308
  80.8 6.0 %collective-permute-start.17 = (bf16[96,768]{1,0:T(8,128)(2,1)S(1)}, bf16[96,768]{1,0:T(8,128)(2,1)S(1)}, u32[]{:S(2)}, u32[]{:S(2)}) collective-permute-start(bf16[96,768]{1,0:T(8,128)(2,1)S(1)} %add_convert_fusion.1), channel_id=1, source_target_pairs={{0,16},{1,9},{2,18},{3,11},{4,20},{5,13},{6,22},{7,15},{8,24},{9,1... | collective-permute-start | bytes 442376 | tf_op jit(solution)/shard_map/ppermute | solution.py:198
  82.1 13.9 %copy-start.2 = (bf16[2,64,768]{2,1,0:T(8,128)(2,1)S(1)}, bf16[2,64,768]{2,1,0:T(8,128)(2,1)}, u32[]{:S(2)}) copy-start(bf16[2,64,768]{2,1,0:T(8,128)(2,1)} %forward.1.att_ref) | copy-start | bytes 589828
  86.9 8.9 %collective-permute-start.18 = (bf16[192,768]{1,0:T(8,128)(2,1)S(1)}, bf16[192,768]{1,0:T(8,128)(2,1)S(1)}, u32[]{:S(2)}, u32[]{:S(2)}) collective-permute-start(bf16[192,768]{1,0:T(8,128)(2,1)S(1)} %bitcast_select_fusion.2), channel_id=1, source_target_pairs={{0,8},{1,17},{2,10},{3,19},{4,12},{5,21},{6,14},{7,23},{8,0},{9,25... | collective-permute-start | bytes 884744 | tf_op jit(solution)/shard_map/ppermute | solution.py:198
  89.3 7.7 %collective-permute-start.10 = (bf16[2,64,768]{2,1,0:T(8,128)(2,1)S(1)}, bf16[2,64,768]{2,1,0:T(8,128)(2,1)S(1)}, u32[]{:S(2)}, u32[]{:S(2)}) collective-permute-start(bf16[2,64,768]{2,1,0:T(8,128)(2,1)S(1)} %get-tuple-element.24), channel_id=1, source_target_pairs={{8,16},{16,8},{9,17},{17,9},{10,18},{18,10},{11,19},{19,11},{12,20... | collective-permute-start | bytes 589832 | tf_op jit(solution)/shard_map/ppermute | solution.py:313
  90.0 10.0 %collective-permute-start.9 = (bf16[2,64,768]{2,1,0:T(8,128)(2,1)S(1)}, bf16[2,64,768]{2,1,0:T(8,128)(2,1)S(1)}, u32[]{:S(2)}, u32[]{:S(2)}) collective-permute-start(bf16[2,64,768]{2,1,0:T(8,128)(2,1)S(1)} %get-tuple-element.23), channel_id=1, source_target_pairs={{0,8},{16,24},{8,0},{24,16},{1,9},{17,25},{9,1},{25,17},{2,10},{18... | collective-permute-start | bytes 589832 | tf_op jit(solution)/shard_map/ppermute | solution.py:312
  95.9 4.1 %copy-start.9 = (f32[2,2,64,768]{3,2,1,0:T(8,128)S(1)}, f32[2,2,64,768]{3,2,1,0:T(8,128)}, u32[]{:S(2)}) copy-start(f32[2,2,64,768]{3,2,1,0:T(8,128)} %get-tuple-element.14) | copy-start | bytes 2359300
  95.9 6.2 %collective-permute-start.19 = (bf16[384,768]{1,0:T(8,128)(2,1)S(1)}, bf16[384,768]{1,0:T(8,128)(2,1)S(1)}, u32[]{:S(2)}, u32[]{:S(2)}) collective-permute-start(bf16[384,768]{1,0:T(8,128)(2,1)S(1)} %bitcast_select_fusion.1), channel_id=1, source_target_pairs={{0,1},{2,3},{4,5},{6,7},{1,0},{3,2},{5,4},{7,6},{8,9},{10,11},{12,... | collective-permute-start | bytes 1769480 | tf_op jit(solution)/shard_map/ppermute | solution.py:230

commit v2 on v1

v2 whole, which is shorter than its diff:
```python
import functools
import math

import jax
import jax.numpy as jnp
from jax import lax
from jax.experimental import pallas as pl
from jax.experimental.pallas import tpu as pltpu
from jax.sharding import PartitionSpec as P


HEAD_DIM = 64
BLK = 8
INNER = BLK * BLK
SLOTS = 4
PAIR = 2 * HEAD_DIM
STAT = 16
NEG = -1e30
BOTH = ("lat", "lon")

VMEM = pl.BlockSpec(memory_space=pltpu.VMEM)
SMEM = pl.BlockSpec(memory_space=pltpu.SMEM)


def swap(pairs):
    return [(a, b) for a, b in pairs] + [(b, a) for a, b in pairs]


def places_of(info, nb, lon_total, neighbours):
    lat_index, lon_index = info[0], info[1]
    even = lax.rem(lon_index, 2) == 0
    places = []
    for q in range(nb):
        row = []
        for s in range(SLOTS):
            block = neighbours[lat_index * nb + q, lon_index, s]
            lat_block = block // lon_total
            lon_block = block - lat_block * lon_total
            right = lon_block == lax.rem(lon_index + 1, lon_total)
            side = jnp.where(right == even, 1, 2)
            column = jnp.where(lon_block == lon_index, 0, side)
            row.append(column * (nb + 2) + lat_block - lat_index * nb + 1)
        places.append(row)
    return places


def edge_rows(info, nb):
    even = lax.rem(info[0], 2) == 0
    return jnp.where(even, nb + 1, 0), jnp.where(even, 0, nb + 1)


def fill(ext, info, nb, parts):
    own, side_a, side_b, edge_e, edge_f, *corners = parts
    if len(corners) == 2:
        corners = [corner.at[k] for corner in corners for k in range(2)]
    e_a, f_a, e_b, f_b = corners
    row_e, row_f = edge_rows(info, nb)
    step = nb + 2
    for i in range(ext.shape[0]):
        for column, rows, e, f in (
            (0, own, edge_e, edge_f),
            (step, side_a, e_a, f_a),
            (2 * step, side_b, e_b, f_b),
        ):
            for r in range(nb):
                ext[i, column + r + 1] = rows[i, r]
            ext[i, column + row_e] = e[i]
            ext[i, column + row_f] = f[i]


def head_masks(value):
    low = lax.broadcasted_iota(jnp.int32, (INNER, PAIR), 1) < HEAD_DIM
    return (
        jnp.where(low, value, 0.0).astype(jnp.bfloat16),
        jnp.where(low, 0.0, value).astype(jnp.bfloat16),
        low,
    )


def two_heads(x, masks):
    return jnp.concatenate([x * masks[0], x * masks[1]], axis=0)


def dot(a, b, dims):
    return lax.dot_general(a, b, (dims, ((), ())), preferred_element_type=jnp.float32)


def probabilities(q2, keys, valid):
    scores = jnp.where(valid, dot(q2, keys, ((1,), (1,))), NEG)
    top = jnp.max(scores, axis=1, keepdims=True)
    weight = jnp.exp(scores - top)
    return weight / jnp.sum(weight, axis=1, keepdims=True)


def key_set(ext, kv, places, cols):
    return jnp.concatenate([ext[kv, place, :, cols] for place in places], axis=0)


def pack_kernel(info, k_ref, v_ref, kv_ref, e_ref, f_ref):
    nb = k_ref.shape[0]
    edge = jnp.where(lax.rem(info[0], 2) == 0, nb - 1, 0)
    for i, ref in enumerate((k_ref, v_ref)):
        kv_ref[i] = ref[...]
        e_ref[i] = ref[edge]
        f_ref[i] = ref[nb - 1 - edge]


def project_kernel(info, q_ref, up_ref, w_ref, qd_ref, e_ref, f_ref):
    nb = q_ref.shape[0]
    edge = jnp.where(lax.rem(info[0], 2) == 0, nb - 1, 0)
    qd_ref[0] = q_ref[...]
    up = up_ref[...].reshape(nb * INNER, -1)
    d_att = dot(up, w_ref[...], ((1,), (1,))).astype(jnp.bfloat16)
    qd_ref[1] = d_att.reshape(nb, INNER, -1)
    for i in range(2):
        e_ref[i] = qd_ref[i, edge]
        f_ref[i] = qd_ref[i, nb - 1 - edge]


def key_slots():
    return lax.broadcasted_iota(jnp.int32, (2 * INNER, SLOTS * INNER), 1) // INNER


def forward_kernel(nb, lon_total, info, neighbours, counts, qd_ref, *refs):
    *inputs, att_ref, stats_ref, ext = refs
    fill(ext, info, nb, inputs)
    places = places_of(info, nb, lon_total, neighbours)
    masks = head_masks(1.0 / math.sqrt(HEAD_DIM))
    low, slot = masks[2], key_slots()
    lane = lax.broadcasted_iota(jnp.int32, (2 * INNER, PAIR), 1)
    stats = jnp.zeros((2 * INNER, PAIR), jnp.float32)
    for q in range(nb):
        valid = slot < counts[info[0] * nb + q, info[1]]
        for p in range(qd_ref.shape[-1] // PAIR):
            cols = slice(p * PAIR, (p + 1) * PAIR)
            q2 = two_heads(qd_ref[0, q, :, cols], masks)
            scores = dot(q2, key_set(ext, 0, places[q], cols), ((1,), (1,)))
            scores = jnp.where(valid, scores, NEG)
            top = jnp.max(scores, axis=1, keepdims=True)
            weight = jnp.exp(scores - top)
            total = jnp.sum(weight, axis=1, keepdims=True)
            probs = (weight / total).astype(jnp.bfloat16)
            mixed = dot(probs, key_set(ext, 1, places[q], cols), ((1,), (0,)))
            att = jnp.where(low, mixed[:INNER], mixed[INNER:]).astype(jnp.bfloat16)
            att_ref[q, :, cols] = att
            product = qd_ref[1, q, :, cols].astype(jnp.float32) * att.astype(jnp.float32)
            delta = row_sums(product, low)
            stats = jnp.where(lane == q * STAT + p, top + jnp.log(total), stats)
            stats = jnp.where(lane == q * STAT + STAT // 2 + p, delta, stats)
    flipped = stats.T
    for q in range(nb):
        stats_ref[0, q] = flipped[q * STAT : (q + 1) * STAT]


def row_sums(product, low):
    return jnp.concatenate(
        [
            jnp.sum(jnp.where(low, product, 0.0), axis=1, keepdims=True),
            jnp.sum(jnp.where(low, 0.0, product), axis=1, keepdims=True),
        ],
        axis=0,
    )


def query_kernel(nb, lon_total, info, neighbours, counts, qd_ref, att_ref, *refs):
    *inputs, dq_ref, ext = refs
    fill(ext, info, nb, inputs)
    places = places_of(info, nb, lon_total, neighbours)
    scale = 1.0 / math.sqrt(HEAD_DIM)
    masks, ones = head_masks(scale), head_masks(1.0)
    low, slot = masks[2], key_slots()
    for q in range(nb):
        valid = slot < counts[info[0] * nb + q, info[1]]
        for p in range(qd_ref.shape[-1] // PAIR):
            cols = slice(p * PAIR, (p + 1) * PAIR)
            q2 = two_heads(qd_ref[0, q, :, cols], masks)
            keys = key_set(ext, 0, places[q], cols)
            values = key_set(ext, 1, places[q], cols)
            probs = probabilities(q2, keys, valid)
            da = qd_ref[1, q, :, cols]
            product = da.astype(jnp.float32) * att_ref[q, :, cols].astype(jnp.float32)
            dprobs = dot(two_heads(da, ones), values, ((1,), (1,)))
            dscores = (probs * (dprobs - row_sums(product, low))).astype(jnp.bfloat16)
            dq2 = dot(dscores, keys, ((1,), (0,)))
            dq_ref[q, :, cols] = (jnp.where(low, dq2[:INNER], dq2[INNER:]) * scale).astype(
                jnp.bfloat16
            )


def key_kernel(nb, lon_total, info, neighbours, counts, kv_ref, *refs):
    *inputs, dk_ref, dv_ref, ext, stats, acc = refs
    fill(ext, info, nb, inputs[:7])
    fill(stats, info, nb, inputs[7:])
    masks, ones = head_masks(1.0 / math.sqrt(HEAD_DIM)), head_masks(1.0)
    lat_index, lon_index = info[0], info[1]
    lat_total = neighbours.shape[0]
    forward = jnp.where(lax.rem(lon_index, 2) == 0, 1, lon_total - 1)
    acc[...] = jnp.zeros_like(acc)
    columns = 3 if lon_total > 2 else 2

    def visit(n, carry):
        r = n // (3 * columns)
        place = n - r * (3 * columns)
        column = place // 3
        row = r + place - column * 3
        shift = jnp.where(column == 0, 0, jnp.where(column == 1, forward, lon_total - forward))
        lon_block = lax.rem(lon_index + shift, lon_total)
        lat_block = lat_index * nb + row - 1
        safe = jnp.clip(lat_block, 0, lat_total - 1)
        key_id = (lat_index * nb + r) * lon_total + lon_index
        limit = counts[safe, lon_block]
        hit = neighbours[safe, lon_block, 0] == key_id
        for s in range(1, SLOTS):
            hit |= (neighbours[safe, lon_block, s] == key_id) & (s < limit)

        @pl.when(hit & (safe == lat_block))
        def _():
            index = column * (nb + 2) + row
            for p in range(kv_ref.shape[-1] // PAIR):
                cols = slice(p * PAIR, (p + 1) * PAIR)
                q2 = two_heads(ext[0, index, :, cols], masks)
                da2 = two_heads(ext[1, index, :, cols], ones)
                scores = dot(kv_ref[0, r, :, cols], q2, ((1,), (1,)))
                probs = jnp.exp(scores - stats[0, index, p : p + 1, :])
                dprobs = dot(kv_ref[1, r, :, cols], da2, ((1,), (1,)))
                delta = stats[0, index, STAT // 2 + p : STAT // 2 + p + 1, :]
                dscores = (probs * (dprobs - delta)).astype(jnp.bfloat16)
                acc[0, r, :, cols] += dot(dscores, q2, ((1,), (0,)))
                acc[1, r, :, cols] += dot(probs.astype(jnp.bfloat16), da2, ((1,), (0,)))

        return carry

    lax.fori_loop(0, nb * 3 * columns, visit, 0)
    dk_ref[...] = acc[0].astype(jnp.bfloat16)
    dv_ref[...] = acc[1].astype(jnp.bfloat16)


def weight_kernel(info, att_own, att_other, up_own, up_other, send_ref, keep_ref):
    half = att_own.shape[1] // 2
    cols = pl.ds(pl.multiple_of(lax.rem(info[1], 2) * half, half), half)
    total = dot(att_own[:, cols], up_own[...], ((0,), (0,)))
    total += dot(att_other[:, cols], up_other[...], ((0,), (0,)))
    rows = half // 2
    first = info[2] == 0
    keep_ref[...] = jnp.where(first, total[:rows], total[rows:])
    send_ref[...] = jnp.where(first, total[rows:], total[:rows]).astype(jnp.bfloat16)


def finish_kernel(scale, info, own_ref, other_ref, out_ref):
    half = own_ref.shape[0]
    core = lax.rem(info[1], 2)
    for ref, at in ((own_ref, core), (other_ref, 1 - core)):
        rows = pl.ds(pl.multiple_of(at * half, half), half)
        out_ref[rows, :] = ref[...].astype(jnp.float32) * scale


def flips(size):
    assert size & (size - 1) == 0
    return [1 << k for k in range(size.bit_length() - 1)]


def lat_sides(lat_size):
    bits = flips(lat_size)
    lat_index, core = lax.axis_index("lat"), lax.axis_index("lon") % 2
    return [
        (lat_index // jnp.where(core == 0, one, two)) % 2 for one, two in zip(bits, bits[::-1])
    ]


def sum_over_mesh(info, sides, att, upstream, up_other, att_other, lat_size, lon_size, scale):
    lat_flips, lon_flips = flips(lat_size), flips(lon_size)[1:]
    lat_orders = (lat_flips, lat_flips[::-1])
    lon_orders = (lon_flips, lon_flips[::-1])

    def exchange(value, step, on_lat):
        pairs = []
        for a in range(lat_size):
            for o in range(lon_size):
                if on_lat:
                    to = (a ^ lat_orders[o % 2][step], o)
                else:
                    to = (a, o ^ lon_orders[o % 2][step])
                pairs.append((a * lon_size + o, to[0] * lon_size + to[1]))
        return lax.ppermute(value, BOTH, pairs)

    width = att.shape[1]
    rows = width // 4
    send, total = pl.pallas_call(
        weight_kernel,
        out_shape=(
            jax.ShapeDtypeStruct((rows, width), jnp.bfloat16),
            jax.ShapeDtypeStruct((rows, width), jnp.float32),
        ),
        in_specs=[SMEM] + [VMEM] * 4,
        out_specs=(VMEM, VMEM),
        name="weight",
    )(info, att, att_other, upstream, up_other)
    got = exchange(send, 0, True)
    for step in range(1, len(lat_flips)):
        total = total + got.astype(jnp.float32)
        halves = total.reshape(2, -1, width)
        total = lax.dynamic_index_in_dim(halves, sides[step], 0, keepdims=False)
        send = lax.dynamic_index_in_dim(halves, 1 - sides[step], 0, keepdims=False)
        got = exchange(send.astype(jnp.bfloat16), step, True)
    low = (total + got.astype(jnp.float32)).astype(jnp.bfloat16)
    for step in range(len(lon_flips)):
        got = exchange(low, step, False)
        low = (low.astype(jnp.float32) + got.astype(jnp.float32)).astype(jnp.bfloat16)
    for step in reversed(range(len(lat_flips))):
        got = exchange(low, step, True)
        mine = lax.broadcasted_iota(jnp.int32, (2, 1, 1), 0) == sides[step]
        low = jnp.where(mine, low[None], got[None]).reshape(-1, width)
    other = lax.ppermute(low, "lon", swap([(o, o + 1) for o in range(0, lon_size, 2)]))
    return pl.pallas_call(
        functools.partial(finish_kernel, scale),
        out_shape=jax.ShapeDtypeStruct((width, width), jnp.float32),
        in_specs=[SMEM, VMEM, VMEM],
        out_specs=VMEM,
        name="finish",
    )(info, low, other)


def layer(queries, key_vectors, value_vectors, upstream, w_out, neighbours, counts):
    lat_rows, lon_cols, width = queries.shape
    assert lon_cols == BLK
    nb = lat_rows // BLK
    lat_size, lon_size = lax.axis_size("lat"), lax.axis_size("lon")
    lon_total = neighbours.shape[1]
    pairs_a = swap([(o, o + 1) for o in range(0, lon_size, 2)])
    pairs_b = swap([(o, (o + 1) % lon_size) for o in range(1, lon_size, 2)])
    pairs_e = swap([(a, a + 1) for a in range(0, lat_size, 2)])
    pairs_f = swap([(a, a + 1) for a in range(1, lat_size - 1, 2)])
    low, full = jnp.bfloat16, jnp.float32
    blocks = (nb, INNER, width)

    def spread(own, to_e, to_f, joined=True):
        side_b = lax.ppermute(own, "lon", pairs_b)
        edge_e = lax.ppermute(to_e, "lat", pairs_e)
        edge_f = lax.ppermute(to_f, "lat", pairs_f)
        side_a = lax.ppermute(own, "lon", pairs_a)
        if joined:
            edges = jnp.stack([edge_e, edge_f])
            corner_b = lax.ppermute(edges, "lon", pairs_b)
            corner_a = lax.ppermute(edges, "lon", pairs_a)
            return (own, side_a, side_b, edge_e, edge_f, corner_a, corner_b)
        e_b = lax.ppermute(edge_e, "lon", pairs_b)
        f_b = lax.ppermute(edge_f, "lon", pairs_b)
        e_a = lax.ppermute(edge_e, "lon", pairs_a)
        f_a = lax.ppermute(edge_f, "lon", pairs_a)
        return (own, side_a, side_b, edge_e, edge_f, e_a, f_a, e_b, f_b)

    sides = lat_sides(lat_size)
    info = jnp.stack([lax.axis_index("lat"), lax.axis_index("lon"), sides[0]]).astype(jnp.int32)
    packed = (
        jax.ShapeDtypeStruct((2,) + blocks, low),
        jax.ShapeDtypeStruct((2,) + blocks[1:], low),
        jax.ShapeDtypeStruct((2,) + blocks[1:], low),
    )
    kv = pl.pallas_call(
        pack_kernel,
        out_shape=packed,
        in_specs=[SMEM, VMEM, VMEM],
        out_specs=(VMEM,) * 3,
        name="pack",
    )(info, key_vectors.reshape(blocks), value_vectors.reshape(blocks))
    kv = spread(*kv, joined=False)
    up_flat = upstream.reshape(-1, width)
    qd = pl.pallas_call(
        project_kernel,
        out_shape=packed,
        in_specs=[SMEM] + [VMEM] * 3,
        out_specs=(VMEM,) * 3,
        name="project",
    )(info, queries.reshape(blocks), upstream.reshape(blocks), w_out)
    up_other = lax.ppermute(up_flat, "lon", pairs_a)
    qd_all = spread(*qd)

    scalars = (info, neighbours, counts)
    ext = pltpu.VMEM((2, 3 * (nb + 2), INNER, width), low)
    att, stats = pl.pallas_call(
        functools.partial(forward_kernel, nb, lon_total),
        out_shape=(
            jax.ShapeDtypeStruct(blocks, low),
            jax.ShapeDtypeStruct((1, nb, STAT, PAIR), full),
        ),
        in_specs=[SMEM] * 3 + [VMEM] * 10,
        out_specs=(VMEM, VMEM),
        scratch_shapes=[ext],
        name="forward",
    )(*scalars, qd[0], *kv)
    att_flat = att.reshape(-1, width)
    att_other = lax.ppermute(att_flat, "lon", pairs_a)
    tokens = lat_rows * lon_cols * lat_size * lon_size
    w_grad = sum_over_mesh(
        info,
        sides,
        att_flat,
        up_flat,
        up_other,
        att_other,
        lat_size,
        lon_size,
        1.0 / math.sqrt(tokens),
    )
    q_grad = pl.pallas_call(
        functools.partial(query_kernel, nb, lon_total),
        out_shape=jax.ShapeDtypeStruct(blocks, low),
        in_specs=[SMEM] * 3 + [VMEM] * 11,
        out_specs=VMEM,
        scratch_shapes=[ext],
        name="query",
    )(*scalars, qd[0], att, *kv)
    mixed = dot(att_flat, w_out, ((1,), (0,))).astype(low)

    edge = jnp.where(lax.axis_index("lat") % 2 == 0, nb - 1, 0)
    stats_e = lax.dynamic_index_in_dim(stats, edge, 1, keepdims=False)
    stats_f = lax.dynamic_index_in_dim(stats, nb - 1 - edge, 1, keepdims=False)
    stats_all = spread(stats, stats_e, stats_f)
    k_grad, v_grad = pl.pallas_call(
        functools.partial(key_kernel, nb, lon_total),
        out_shape=(jax.ShapeDtypeStruct(blocks, low),) * 2,
        in_specs=[SMEM] * 3 + [VMEM] * 15,
        out_specs=(VMEM, VMEM),
        scratch_shapes=[
            ext,
            pltpu.VMEM((1, 3 * (nb + 2), STAT, PAIR), full),
            pltpu.VMEM((2,) + blocks, full),
        ],
        name="keys",
    )(*scalars, kv[0], *qd_all, *stats_all)
    shape = queries.shape
    return (
        mixed.reshape(shape),
        q_grad.reshape(shape),
        k_grad.reshape(shape),
        v_grad.reshape(shape),
        w_grad,
    )


def solution(mesh):
    grid = P("lat", "lon", None)
    return jax.shard_map(
        layer,
        mesh=mesh,
        in_specs=(grid, grid, grid, grid, P(), P(), P()),
        out_specs=(grid, grid, grid, grid, P()),
        check_vma=False,
    )
```

time: 105 us -> 126 us (1.20)
  the two profiles are of different devices: /device:TPU:0 before, /device:TPU:4 now
where the time goes in v2:
time: 126 us; the launch traced here: 125 us
  waiting for transfers between devices  52.2 us (41%)
  Pallas kernels  34.9 us (28%)
  starting transfers between devices  28.2 us (22%)
  other arithmetic  3.93 us (3%)
  local copies, waits for them, and re-layouts  3.75 us (3%)
    ppermute x6, waiting for transfers between devices, exchange(): return lax.ppermute(value, BOTH, pairs)  28.2 us
    pallas_call x1, Pallas kernels, layer(): pl.pallas_call(functools.partial(key_kernel, nb, lon_total), out_shape=(j...  14.2 us
    ppermute x3, waiting for transfers between devices, spread(): side_b = lax.ppermute(own, 'lon', pairs_b)  9.33 us
    ppermute x3, starting transfers between devices, spread(): edge_f = lax.ppermute(to_f, 'lat', pairs_f)  8.86 us
    ppermute x3, waiting for transfers between devices, spread(): edge_f = lax.ppermute(to_f, 'lat', pairs_f)  7.9 us
    ppermute x3, starting transfers between devices, spread(): side_b = lax.ppermute(own, 'lon', pairs_b)  6.46 us
    pallas_call x1, Pallas kernels, layer(): pl.pallas_call(functools.partial(query_kernel, nb, lon_total), out_shape=...  5.61 us
    pallas_call x1, Pallas kernels, layer(): pl.pallas_call(functools.partial(forward_kernel, nb, lon_total), out_shap...  4.69 us
  transfers between devices with their start and end apart: 29, of which 13 were waited for; matrix products, arithmetic and copies ran while one was open for 4% of the time, Pallas kernels for 22%

profile of v2, /device:TPU:4, one launch (start us, length us, event | category | flops | bytes accessed | tf_op | source)
XLA Modules:
  0.0 125.0 jit_solution(6871577059762249673)
XLA Ops:
  1.4 1.9 %pack.1 = (bf16[2,2,64,768]{3,2,1,0:T(8,128)(2,1)}, bf16[2,64,768]{2,1,0:T(8,128)(2,1)}, bf16[2,64,768]{2,1,0:T(8,128)(2,1)}) custom-call(s32[3]{0:T(128)} %pad_add_fusion.info, bf16[2,64,768]{2,1,0:T(8,128)(2,1)} %bitcast.49, bf16[2,64,768]{2,1,0:T(8,128)(2,1)} %bitcast.50), custom_call_target="tpu_custom_call" | custom-call | tf_op jit(solution)/shard_map/pack/pallas_call | solution.py:359
  3.3 3.7 %collective-permute-start.1 = (bf16[2,2,64,768]{3,2,1,0:T(8,128)(2,1)}, bf16[2,2,64,768]{3,2,1,0:T(8,128)(2,1)S(1)}, u32[]{:S(2)}, u32[]{:S(2)}) collective-permute-start(bf16[2,2,64,768]{3,2,1,0:T(8,128)(2,1)} %get-tuple-element.18.refs_0_.kv_ref), channel_id=1, source_target_pairs={{1,2},{3,4},{5,6},{7,0},{2,1},{4,3},{6,5},{0,7},{9,10},{11,12},{13... | collective-permute-start | bytes 1179656 | tf_op jit(solution)/shard_map/ppermute | solution.py:337
  7.0 1.5 %collective-permute-start.2 = (bf16[2,64,768]{2,1,0:T(8,128)(2,1)}, bf16[2,64,768]{2,1,0:T(8,128)(2,1)S(1)}, u32[]{:S(2)}, u32[]{:S(2)}) collective-permute-start(bf16[2,64,768]{2,1,0:T(8,128)(2,1)} %get-tuple-element.19), channel_id=1, source_target_pairs={{0,8},{16,24},{8,0},{24,16},{1,9},{17,25},{9,1},{25,17},{2,10},{18... | collective-permute-start | bytes 589832 | tf_op jit(solution)/shard_map/ppermute | solution.py:338
  8.5 2.4 %collective-permute-start.3 = (bf16[2,64,768]{2,1,0:T(8,128)(2,1)}, bf16[2,64,768]{2,1,0:T(8,128)(2,1)S(1)}, u32[]{:S(2)}, u32[]{:S(2)}) collective-permute-start(bf16[2,64,768]{2,1,0:T(8,128)(2,1)} %get-tuple-element.20), channel_id=1, source_target_pairs={{8,16},{16,8},{9,17},{17,9},{10,18},{18,10},{11,19},{19,11},{12,20... | collective-permute-start | bytes 589832 | tf_op jit(solution)/shard_map/ppermute | solution.py:339
  10.9 2.3 %collective-permute-done.2.refs_3_ = bf16[2,64,768]{2,1,0:T(8,128)(2,1)S(1)} collective-permute-done((bf16[2,64,768]{2,1,0:T(8,128)(2,1)}, bf16[2,64,768]{2,1,0:T(8,128)(2,1)S(1)}, u32[]{:S(2)}, u32[]{:S(2)}) %collective-permute-start.2) | collective-permute-done | bytes 196640 | tf_op jit(solution)/shard_map/ppermute | solution.py:338
  13.2 1.4 %collective-permute-start.6 = (bf16[2,64,768]{2,1,0:T(8,128)(2,1)S(1)}, bf16[2,64,768]{2,1,0:T(8,128)(2,1)S(1)}, u32[]{:S(2)}, u32[]{:S(2)}) collective-permute-start(bf16[2,64,768]{2,1,0:T(8,128)(2,1)S(1)} %collective-permute-done.2.refs_3_), channel_id=1, source_target_pairs={{1,2},{3,4},{5,6},{7,0},{2,1},{4,3},{6,5},{0,7},{9,10},{11,12},{13... | collective-permute-start | bytes 589832 | tf_op jit(solution)/shard_map/ppermute | solution.py:346
  14.7 2.5 %collective-permute-done.3.refs_4_ = bf16[2,64,768]{2,1,0:T(8,128)(2,1)S(1)} collective-permute-done((bf16[2,64,768]{2,1,0:T(8,128)(2,1)}, bf16[2,64,768]{2,1,0:T(8,128)(2,1)S(1)}, u32[]{:S(2)}, u32[]{:S(2)}) %collective-permute-start.3) | collective-permute-done | bytes 196640 | tf_op jit(solution)/shard_map/ppermute | solution.py:339
  17.2 1.5 %collective-permute-start.7 = (bf16[2,64,768]{2,1,0:T(8,128)(2,1)S(1)}, bf16[2,64,768]{2,1,0:T(8,128)(2,1)S(1)}, u32[]{:S(2)}, u32[]{:S(2)}) collective-permute-start(bf16[2,64,768]{2,1,0:T(8,128)(2,1)S(1)} %collective-permute-done.3.refs_4_), channel_id=1, source_target_pairs={{1,2},{3,4},{5,6},{7,0},{2,1},{4,3},{6,5},{0,7},{9,10},{11,12},{13... | collective-permute-start | bytes 589832 | tf_op jit(solution)/shard_map/ppermute | solution.py:347
  18.7 1.4 %copy.12.neighbours = s32[8,8,4]{2,1,0:T(8,128)} copy(s32[8,8,4]{1,2,0:T(4,128)} %param.12) | data formatting | bytes 2048 | tf_op args[5]
  20.1 2.9 %project.1 = (bf16[2,2,64,768]{3,2,1,0:T(8,128)(2,1)}, bf16[2,64,768]{2,1,0:T(8,128)(2,1)}, bf16[2,64,768]{2,1,0:T(8,128)(2,1)}) custom-call(s32[3]{0:T(128)} %pad_add_fusion.info, bf16[2,64,768]{2,1,0:T(8,128)(2,1)} %bitcast.51, bf16[2,64,768]{2,1,0:T(8,128)(2,1)} %bitcast.46, bf16[768,768]{1,0:T(8,128)(2,1)} %w_ref.1), custom_call_target="tpu_custom_call" | custom-call | tf_op jit(solution)/shard_map/project/pallas_call | solution.py:368
  23.2 2.7 %collective-permute-done.7.refs_8_ = bf16[2,64,768]{2,1,0:T(8,128)(2,1)S(1)} collective-permute-done((bf16[2,64,768]{2,1,0:T(8,128)(2,1)S(1)}, bf16[2,64,768]{2,1,0:T(8,128)(2,1)S(1)}, u32[]{:S(2)}, u32[]{:S(2)}) %collective-permute-start.7) | collective-permute-done | bytes 196640 | tf_op jit(solution)/shard_map/ppermute | solution.py:347
  26.6 4.7 %forward.1 = (bf16[2,64,768]{2,1,0:T(8,128)(2,1)}, f32[1,2,16,128]{3,2,1,0:T(8,128)}) custom-call(s32[3]{0:T(128)} %pad_add_fusion.info, s32[8,8,4]{2,1,0:T(8,128)} %copy.12.neighbours, s32[8,8]{1,0:T(8,128)} %counts.5, bf16[2,2,64,768]{3,2,1,0:T(8,128)(2,1)} %get-tuple-element.17.qd_ref.refs_0_, bf16[2,2,64,768]{3,2,1,0:T(8,128)(2,1)} %get-tuple-element.18.refs_0_.kv_ref, ...), custom_call_target="tpu_custom_call" | custom-call | tf_op jit(solution)/shard_map/forward/pallas_call | solution.py:380
  31.3 1.6 %collective-permute-done.20.att_other = bf16[128,768]{1,0:T(8,128)(2,1)S(1)} collective-permute-done((bf16[128,768]{1,0:T(8,128)(2,1)}, bf16[128,768]{1,0:T(8,128)(2,1)S(1)}, u32[]{:S(2)}, u32[]{:S(2)}) %collective-permute-start.20) | collective-permute-done | bytes 196640 | tf_op jit(solution)/shard_map/ppermute | solution.py:392
  33.6 2.6 %weight.1 = (bf16[192,768]{1,0:T(8,128)(2,1)}, f32[192,768]{1,0:T(8,128)}) custom-call(s32[3]{0:T(128)} %pad_add_fusion.info, bf16[128,768]{1,0:T(8,128)(2,1)} %bitcast.42, bf16[128,768]{1,0:T(8,128)(2,1)} %copy-done.17, bf16[128,768]{1,0:T(8,128)(2,1)} %bitcast.47, bf16[128,768]{1,0:T(8,128)(2,1)} %copy-done.16), custom_call_target="tpu_custom_call" | custom-call | tf_op jit(solution)/shard_map/weight/pallas_call | solution.py:288
  36.3 1.5 %collective-permute-start.22 = (bf16[192,768]{1,0:T(8,128)(2,1)}, bf16[192,768]{1,0:T(8,128)(2,1)S(1)}, u32[]{:S(2)}, u32[]{:S(2)}) collective-permute-start(bf16[192,768]{1,0:T(8,128)(2,1)} %get-tuple-element.28), channel_id=1, source_target_pairs={{0,8},{1,17},{2,10},{3,19},{4,12},{5,21},{6,14},{7,23},{8,0},{9,25... | collective-permute-start | bytes 884744 | tf_op jit(solution)/shard_map/ppermute | solution.py:284
  37.7 5.5 %collective-permute-done.22 = bf16[192,768]{1,0:T(8,128)(2,1)S(1)} collective-permute-done((bf16[192,768]{1,0:T(8,128)(2,1)}, bf16[192,768]{1,0:T(8,128)(2,1)S(1)}, u32[]{:S(2)}, u32[]{:S(2)}) %collective-permute-start.22) | collective-permute-done | bytes 294944 | tf_op jit(solution)/shard_map/ppermute | solution.py:284
  44.9 4.6 %collective-permute-done.23 = bf16[96,768]{1,0:T(8,128)(2,1)S(1)} collective-permute-done((bf16[96,768]{1,0:T(8,128)(2,1)S(1)}, bf16[96,768]{1,0:T(8,128)(2,1)S(1)}, u32[]{:S(2)}, u32[]{:S(2)}) %collective-permute-start.23) | collective-permute-done | bytes 147488 | tf_op jit(solution)/shard_map/ppermute | solution.py:284
  49.7 5.7 %collective-permute-done.24 = bf16[96,768]{1,0:T(8,128)(2,1)S(1)} collective-permute-done((bf16[96,768]{1,0:T(8,128)(2,1)S(1)}, bf16[96,768]{1,0:T(8,128)(2,1)S(1)}, u32[]{:S(2)}, u32[]{:S(2)}) %collective-permute-start.24) | collective-permute-done | bytes 147488 | tf_op jit(solution)/shard_map/ppermute | solution.py:284
  55.5 6.6 %collective-permute-done.25 = bf16[96,768]{1,0:T(8,128)(2,1)S(1)} collective-permute-done((bf16[96,768]{1,0:T(8,128)(2,1)S(1)}, bf16[96,768]{1,0:T(8,128)(2,1)S(1)}, u32[]{:S(2)}, u32[]{:S(2)}) %collective-permute-start.25) | collective-permute-done | bytes 147488 | tf_op jit(solution)/shard_map/ppermute | solution.py:284
  63.1 5.8 %collective-permute-done.26 = bf16[96,768]{1,0:T(8,128)(2,1)S(1)} collective-permute-done((bf16[96,768]{1,0:T(8,128)(2,1)S(1)}, bf16[96,768]{1,0:T(8,128)(2,1)S(1)}, u32[]{:S(2)}, u32[]{:S(2)}) %collective-permute-start.26) | collective-permute-done | bytes 147488 | tf_op jit(solution)/shard_map/ppermute | solution.py:284
  69.1 1.5 %collective-permute-start.27 = (bf16[192,768]{1,0:T(8,128)(2,1)S(1)}, bf16[192,768]{1,0:T(8,128)(2,1)}, u32[]{:S(2)}, u32[]{:S(2)}) collective-permute-start(bf16[192,768]{1,0:T(8,128)(2,1)S(1)} %bitcast_select_fusion.1), channel_id=1, source_target_pairs={{0,8},{1,17},{2,10},{3,19},{4,12},{5,21},{6,14},{7,23},{8,0},{9,25... | collective-permute-start | bytes 884744 | tf_op jit(solution)/shard_map/ppermute | solution.py:284
  71.1 3.8 %collective-permute-start.11 = (bf16[2,64,768]{2,1,0:T(8,128)(2,1)}, bf16[2,64,768]{2,1,0:T(8,128)(2,1)S(1)}, u32[]{:S(2)}, u32[]{:S(2)}) collective-permute-start(bf16[2,64,768]{2,1,0:T(8,128)(2,1)} %get-tuple-element.23), channel_id=1, source_target_pairs={{8,16},{16,8},{9,17},{17,9},{10,18},{18,10},{11,19},{19,11},{12,20... | collective-permute-start | bytes 589832 | tf_op jit(solution)/shard_map/ppermute | solution.py:339
  75.0 2.0 %collective-permute-start.9 = (bf16[2,2,64,768]{3,2,1,0:T(8,128)(2,1)S(1)}, bf16[2,2,64,768]{3,2,1,0:T(8,128)(2,1)}, u32[]{:S(2)}, u32[]{:S(2)}) collective-permute-start(bf16[2,2,64,768]{3,2,1,0:T(8,128)(2,1)S(1)} %copy-done.1), channel_id=1, source_target_pairs={{1,2},{3,4},{5,6},{7,0},{2,1},{4,3},{6,5},{0,7},{9,10},{11,12},{13... | collective-permute-start | bytes 1179656 | tf_op jit(solution)/shard_map/ppermute | solution.py:337
  78.5 1.8 %collective-permute-done.11.refs_4_ = bf16[2,64,768]{2,1,0:T(8,128)(2,1)S(1)} collective-permute-done((bf16[2,64,768]{2,1,0:T(8,128)(2,1)}, bf16[2,64,768]{2,1,0:T(8,128)(2,1)S(1)}, u32[]{:S(2)}, u32[]{:S(2)}) %collective-permute-start.11) | collective-permute-done | bytes 196640 | tf_op jit(solution)/shard_map/ppermute | solution.py:339
  81.1 2.0 %collective-permute-start.13 = (bf16[2,2,64,768]{3,2,1,0:T(8,128)(2,1)}, bf16[2,2,64,768]{3,2,1,0:T(8,128)(2,1)}, u32[]{:S(2)}, u32[]{:S(2)}) collective-permute-start(bf16[2,2,64,768]{3,2,1,0:T(8,128)(2,1)} %pad_maximum_fusion), channel_id=1, source_target_pairs={{1,2},{3,4},{5,6},{7,0},{2,1},{4,3},{6,5},{0,7},{9,10},{11,12},{13... | collective-permute-start | bytes 1179656 | tf_op jit(solution)/shard_map/ppermute | solution.py:343
  83.3 5.2 %collective-permute-done.9.refs_2_ = bf16[2,2,64,768]{3,2,1,0:T(8,128)(2,1)} collective-permute-done((bf16[2,2,64,768]{3,2,1,0:T(8,128)(2,1)S(1)}, bf16[2,2,64,768]{3,2,1,0:T(8,128)(2,1)}, u32[]{:S(2)}, u32[]{:S(2)}) %collective-permute-start.9) | collective-permute-done | bytes 393248 | tf_op jit(solution)/shard_map/ppermute | solution.py:337
  88.4 2.7 %collective-permute-start.17 = (f32[1,16,128]{2,1,0:T(8,128)S(1)}, f32[1,16,128]{2,1,0:T(8,128)S(1)}, u32[]{:S(2)}, u32[]{:S(2)}) collective-permute-start(f32[1,16,128]{2,1,0:T(8,128)S(1)} %get-tuple-element.29), channel_id=1, source_target_pairs={{8,16},{16,8},{9,17},{17,9},{10,18},{18,10},{11,19},{19,11},{12,20... | collective-permute-start | bytes 24584 | tf_op jit(solution)/shard_map/ppermute | solution.py:339
  91.2 3.6 %collective-permute-done.17.refs_11_ = f32[1,16,128]{2,1,0:T(8,128)S(1)} collective-permute-done((f32[1,16,128]{2,1,0:T(8,128)S(1)}, f32[1,16,128]{2,1,0:T(8,128)S(1)}, u32[]{:S(2)}, u32[]{:S(2)}) %collective-permute-start.17) | collective-permute-done | bytes 8224 | tf_op jit(solution)/shard_map/ppermute | solution.py:339
  95.7 4.2 %collective-permute-done.15.refs_9_ = f32[1,2,16,128]{3,2,1,0:T(8,128)S(1)} collective-permute-done((f32[1,2,16,128]{3,2,1,0:T(8,128)S(1)}, f32[1,2,16,128]{3,2,1,0:T(8,128)S(1)}, u32[]{:S(2)}, u32[]{:S(2)}) %collective-permute-start.15) | collective-permute-done | bytes 16416 | tf_op jit(solution)/shard_map/ppermute | solution.py:337
  101.6 5.6 %query.1 = bf16[2,64,768]{2,1,0:T(8,128)(2,1)} custom-call(s32[3]{0:T(128)} %pad_add_fusion.info, s32[8,8,4]{2,1,0:T(8,128)} %copy.12.neighbours, s32[8,8]{1,0:T(8,128)} %counts.5, bf16[2,2,64,768]{3,2,1,0:T(8,128)(2,1)} %get-tuple-element.17.qd_ref.refs_0_, bf16[2,64,768]{2,1,0:T(8,128)(2,1)} %get-tuple-element.21.att_ref, ...), custom_call_target="tpu_custom_call" | custom-call | tf_op jit(solution)/shard_map/query/pallas_call | solution.py:405
  107.9 14.2 %keys.1 = (bf16[2,64,768]{2,1,0:T(8,128)(2,1)}, bf16[2,64,768]{2,1,0:T(8,128)(2,1)}) custom-call(s32[3]{0:T(128)} %pad_add_fusion.info, s32[8,8,4]{2,1,0:T(8,128)} %copy.12.neighbours, s32[8,8]{1,0:T(8,128)} %counts.5, bf16[2,2,64,768]{3,2,1,0:T(8,128)(2,1)} %get-tuple-element.18.refs_0_.kv_ref, bf16[2,2,64,768]{3,2,1,0:T(8,128)(2,1)} %get-tuple-element.17.qd_ref.refs_0_, ...), custom_call_target="tpu_custom_call" | custom-call | tf_op jit(solution)/shard_map/keys/pallas_call | solution.py:419
  122.2 2.8 %finish.1 = f32[768,768]{1,0:T(8,128)} custom-call(s32[3]{0:T(128)} %pad_add_fusion.info, bf16[384,768]{1,0:T(8,128)(2,1)} %copy-done.2, bf16[384,768]{1,0:T(8,128)(2,1)} %collective-permute-done.28.other_ref), custom_call_target="tpu_custom_call" | custom-call | tf_op jit(solution)/shard_map/finish/pallas_call | solution.py:314
  (102 shorter events, 11.4 us)
Async XLA Ops:
  3.3 13.9 %collective-permute-start = (bf16[2,2,64,768]{3,2,1,0:T(8,128)(2,1)}, bf16[2,2,64,768]{3,2,1,0:T(8,128)(2,1)S(1)}, u32[]{:S(2)}, u32[]{:S(2)}) collective-permute-start(bf16[2,2,64,768]{3,2,1,0:T(8,128)(2,1)} %get-tuple-element.18.refs_0_.kv_ref), channel_id=1, source_target_pairs={{0,1},{2,3},{4,5},{6,7},{1,0},{3,2},{5,4},{7,6},{8,9},{10,11},{12,... | collective-permute-start | bytes 1179656 | tf_op jit(solution)/shard_map/ppermute | solution.py:340
  3.3 19.8 %collective-permute-start.1 = (bf16[2,2,64,768]{3,2,1,0:T(8,128)(2,1)}, bf16[2,2,64,768]{3,2,1,0:T(8,128)(2,1)S(1)}, u32[]{:S(2)}, u32[]{:S(2)}) collective-permute-start(bf16[2,2,64,768]{3,2,1,0:T(8,128)(2,1)} %get-tuple-element.18.refs_0_.kv_ref), channel_id=1, source_target_pairs={{1,2},{3,4},{5,6},{7,0},{2,1},{4,3},{6,5},{0,7},{9,10},{11,12},{13... | collective-permute-start | bytes 1179656 | tf_op jit(solution)/shard_map/ppermute | solution.py:337
  7.0 6.2 %collective-permute-start.2 = (bf16[2,64,768]{2,1,0:T(8,128)(2,1)}, bf16[2,64,768]{2,1,0:T(8,128)(2,1)S(1)}, u32[]{:S(2)}, u32[]{:S(2)}) collective-permute-start(bf16[2,64,768]{2,1,0:T(8,128)(2,1)} %get-tuple-element.19), channel_id=1, source_target_pairs={{0,8},{16,24},{8,0},{24,16},{1,9},{17,25},{9,1},{25,17},{2,10},{18... | collective-permute-start | bytes 589832 | tf_op jit(solution)/shard_map/ppermute | solution.py:338
  8.5 8.7 %collective-permute-start.3 = (bf16[2,64,768]{2,1,0:T(8,128)(2,1)}, bf16[2,64,768]{2,1,0:T(8,128)(2,1)S(1)}, u32[]{:S(2)}, u32[]{:S(2)}) collective-permute-start(bf16[2,64,768]{2,1,0:T(8,128)(2,1)} %get-tuple-element.20), channel_id=1, source_target_pairs={{8,16},{16,8},{9,17},{17,9},{10,18},{18,10},{11,19},{19,11},{12,20... | collective-permute-start | bytes 589832 | tf_op jit(solution)/shard_map/ppermute | solution.py:339
  13.2 9.9 %collective-permute-start.4 = (bf16[2,64,768]{2,1,0:T(8,128)(2,1)S(1)}, bf16[2,64,768]{2,1,0:T(8,128)(2,1)S(1)}, u32[]{:S(2)}, u32[]{:S(2)}) collective-permute-start(bf16[2,64,768]{2,1,0:T(8,128)(2,1)S(1)} %collective-permute-done.2.refs_3_), channel_id=1, source_target_pairs={{0,1},{2,3},{4,5},{6,7},{1,0},{3,2},{5,4},{7,6},{8,9},{10,11},{12,... | collective-permute-start | bytes 589832 | tf_op jit(solution)/shard_map/ppermute | solution.py:348
  13.2 10.0 %collective-permute-start.6 = (bf16[2,64,768]{2,1,0:T(8,128)(2,1)S(1)}, bf16[2,64,768]{2,1,0:T(8,128)(2,1)S(1)}, u32[]{:S(2)}, u32[]{:S(2)}) collective-permute-start(bf16[2,64,768]{2,1,0:T(8,128)(2,1)S(1)} %collective-permute-done.2.refs_3_), channel_id=1, source_target_pairs={{1,2},{3,4},{5,6},{7,0},{2,1},{4,3},{6,5},{0,7},{9,10},{11,12},{13... | collective-permute-start | bytes 589832 | tf_op jit(solution)/shard_map/ppermute | solution.py:346
  17.2 6.0 %collective-permute-start.5 = (bf16[2,64,768]{2,1,0:T(8,128)(2,1)S(1)}, bf16[2,64,768]{2,1,0:T(8,128)(2,1)S(1)}, u32[]{:S(2)}, u32[]{:S(2)}) collective-permute-start(bf16[2,64,768]{2,1,0:T(8,128)(2,1)S(1)} %collective-permute-done.3.refs_4_), channel_id=1, source_target_pairs={{0,1},{2,3},{4,5},{6,7},{1,0},{3,2},{5,4},{7,6},{8,9},{10,11},{12,... | collective-permute-start | bytes 589832 | tf_op jit(solution)/shard_map/ppermute | solution.py:349
  17.2 8.7 %collective-permute-start.7 = (bf16[2,64,768]{2,1,0:T(8,128)(2,1)S(1)}, bf16[2,64,768]{2,1,0:T(8,128)(2,1)S(1)}, u32[]{:S(2)}, u32[]{:S(2)}) collective-permute-start(bf16[2,64,768]{2,1,0:T(8,128)(2,1)S(1)} %collective-permute-done.3.refs_4_), channel_id=1, source_target_pairs={{1,2},{3,4},{5,6},{7,0},{2,1},{4,3},{6,5},{0,7},{9,10},{11,12},{13... | collective-permute-start | bytes 589832 | tf_op jit(solution)/shard_map/ppermute | solution.py:347
  23.1 8.2 %collective-permute-start.21 = (bf16[128,768]{1,0:T(8,128)(2,1)S(1)}, bf16[128,768]{1,0:T(8,128)(2,1)S(1)}, u32[]{:S(2)}, u32[]{:S(2)}) collective-permute-start(bf16[128,768]{1,0:T(8,128)(2,1)S(1)} %bitcast.48), channel_id=1, source_target_pairs={{0,1},{2,3},{4,5},{6,7},{1,0},{3,2},{5,4},{7,6},{8,9},{10,11},{12,... | collective-permute-start | bytes 589832 | tf_op jit(solution)/shard_map/ppermute | solution.py:375
  31.3 1.7 %collective-permute-start.20 = (bf16[128,768]{1,0:T(8,128)(2,1)}, bf16[128,768]{1,0:T(8,128)(2,1)S(1)}, u32[]{:S(2)}, u32[]{:S(2)}) collective-permute-start(bf16[128,768]{1,0:T(8,128)(2,1)} %bitcast.41), channel_id=1, source_target_pairs={{0,1},{2,3},{4,5},{6,7},{1,0},{3,2},{5,4},{7,6},{8,9},{10,11},{12,... | collective-permute-start | bytes 589832 | tf_op jit(solution)/shard_map/ppermute | solution.py:392
  36.3 6.9 %collective-permute-start.22 = (bf16[192,768]{1,0:T(8,128)(2,1)}, bf16[192,768]{1,0:T(8,128)(2,1)S(1)}, u32[]{:S(2)}, u32[]{:S(2)}) collective-permute-start(bf16[192,768]{1,0:T(8,128)(2,1)} %get-tuple-element.28), channel_id=1, source_target_pairs={{0,8},{1,17},{2,10},{3,19},{4,12},{5,21},{6,14},{7,23},{8,0},{9,25... | collective-permute-start | bytes 884744 | tf_op jit(solution)/shard_map/ppermute | solution.py:284
  44.3 30.6 %copy-start.1 = (bf16[2,2,64,768]{3,2,1,0:T(8,128)(2,1)S(1)}, bf16[2,2,64,768]{3,2,1,0:T(8,128)(2,1)}, u32[]{:S(2)}) copy-start(bf16[2,2,64,768]{3,2,1,0:T(8,128)(2,1)} %get-tuple-element.17.qd_ref.refs_0_) | copy-start | bytes 1179652
  44.4 5.2 %collective-permute-start.23 = (bf16[96,768]{1,0:T(8,128)(2,1)S(1)}, bf16[96,768]{1,0:T(8,128)(2,1)S(1)}, u32[]{:S(2)}, u32[]{:S(2)}) collective-permute-start(bf16[96,768]{1,0:T(8,128)(2,1)S(1)} %fusion.2), channel_id=1, source_target_pairs={{0,16},{1,9},{2,18},{3,11},{4,20},{5,13},{6,22},{7,15},{8,24},{9,1... | collective-permute-start | bytes 442376 | tf_op jit(solution)/shard_map/ppermute | solution.py:284
  49.6 5.8 %collective-permute-start.24 = (bf16[96,768]{1,0:T(8,128)(2,1)S(1)}, bf16[96,768]{1,0:T(8,128)(2,1)S(1)}, u32[]{:S(2)}, u32[]{:S(2)}) collective-permute-start(bf16[96,768]{1,0:T(8,128)(2,1)S(1)} %fusion.1), channel_id=1, source_target_pairs={{0,2},{1,5},{2,0},{3,7},{4,6},{5,1},{6,4},{7,3},{8,10},{9,13},{10,... | collective-permute-start | bytes 442376 | tf_op jit(solution)/shard_map/ppermute | solution.py:284
  55.4 6.7 %collective-permute-start.25 = (bf16[96,768]{1,0:T(8,128)(2,1)S(1)}, bf16[96,768]{1,0:T(8,128)(2,1)S(1)}, u32[]{:S(2)}, u32[]{:S(2)}) collective-permute-start(bf16[96,768]{1,0:T(8,128)(2,1)S(1)} %add_convert_fusion.1), channel_id=1, source_target_pairs={{0,4},{1,3},{2,6},{3,1},{4,0},{5,7},{6,2},{7,5},{8,12},{9,11},{10,... | collective-permute-start | bytes 442376 | tf_op jit(solution)/shard_map/ppermute | solution.py:284
  62.1 6.8 %collective-permute-start.26 = (bf16[96,768]{1,0:T(8,128)(2,1)S(1)}, bf16[96,768]{1,0:T(8,128)(2,1)S(1)}, u32[]{:S(2)}, u32[]{:S(2)}) collective-permute-start(bf16[96,768]{1,0:T(8,128)(2,1)S(1)} %add_convert_fusion), channel_id=1, source_target_pairs={{0,16},{1,9},{2,18},{3,11},{4,20},{5,13},{6,22},{7,15},{8,24},{9,1... | collective-permute-start | bytes 442376 | tf_op jit(solution)/shard_map/ppermute | solution.py:284
  69.0 31.6 %copy-start = (bf16[768,768]{1,0:T(8,128)(2,1)S(1)}, bf16[768,768]{1,0:T(8,128)(2,1)}, u32[]{:S(2)}) copy-start(bf16[768,768]{1,0:T(8,128)(2,1)} %w_ref.1) | copy-start | bytes 3538948
  69.0 31.6 %copy-start.3 = (bf16[2,64,768]{2,1,0:T(8,128)(2,1)S(1)}, bf16[2,64,768]{2,1,0:T(8,128)(2,1)}, u32[]{:S(2)}) copy-start(bf16[2,64,768]{2,1,0:T(8,128)(2,1)} %get-tuple-element.21.att_ref) | copy-start | bytes 589828
  69.1 8.2 %collective-permute-start.27 = (bf16[192,768]{1,0:T(8,128)(2,1)S(1)}, bf16[192,768]{1,0:T(8,128)(2,1)}, u32[]{:S(2)}, u32[]{:S(2)}) collective-permute-start(bf16[192,768]{1,0:T(8,128)(2,1)S(1)} %bitcast_select_fusion.1), channel_id=1, source_target_pairs={{0,8},{1,17},{2,10},{3,19},{4,12},{5,21},{6,14},{7,23},{8,0},{9,25... | collective-permute-start | bytes 884744 | tf_op jit(solution)/shard_map/ppermute | solution.py:284
  70.6 7.9 %collective-permute-start.10 = (bf16[2,64,768]{2,1,0:T(8,128)(2,1)}, bf16[2,64,768]{2,1,0:T(8,128)(2,1)S(1)}, u32[]{:S(2)}, u32[]{:S(2)}) collective-permute-start(bf16[2,64,768]{2,1,0:T(8,128)(2,1)} %get-tuple-element.22), channel_id=1, source_target_pairs={{0,8},{16,24},{8,0},{24,16},{1,9},{17,25},{9,1},{25,17},{2,10},{18... | collective-permute-start | bytes 589832 | tf_op jit(solution)/shard_map/ppermute | solution.py:338
  71.1 9.1 %collective-permute-start.11 = (bf16[2,64,768]{2,1,0:T(8,128)(2,1)}, bf16[2,64,768]{2,1,0:T(8,128)(2,1)S(1)}, u32[]{:S(2)}, u32[]{:S(2)}) collective-permute-start(bf16[2,64,768]{2,1,0:T(8,128)(2,1)} %get-tuple-element.23), channel_id=1, source_target_pairs={{8,16},{16,8},{9,17},{17,9},{10,18},{18,10},{11,19},{19,11},{12,20... | collective-permute-start | bytes 589832 | tf_op jit(solution)/shard_map/ppermute | solution.py:339
  75.0 8.2 %collective-permute-start.8 = (bf16[2,2,64,768]{3,2,1,0:T(8,128)(2,1)S(1)}, bf16[2,2,64,768]{3,2,1,0:T(8,128)(2,1)S(1)}, u32[]{:S(2)}, u32[]{:S(2)}) collective-permute-start(bf16[2,2,64,768]{3,2,1,0:T(8,128)(2,1)S(1)} %copy-done.1), channel_id=1, source_target_pairs={{0,1},{2,3},{4,5},{6,7},{1,0},{3,2},{5,4},{7,6},{8,9},{10,11},{12,... | collective-permute-start | bytes 1179656 | tf_op jit(solution)/shard_map/ppermute | solution.py:340
  75.0 13.4 %collective-permute-start.9 = (bf16[2,2,64,768]{3,2,1,0:T(8,128)(2,1)S(1)}, bf16[2,2,64,768]{3,2,1,0:T(8,128)(2,1)}, u32[]{:S(2)}, u32[]{:S(2)}) collective-permute-start(bf16[2,2,64,768]{3,2,1,0:T(8,128)(2,1)S(1)} %copy-done.1), channel_id=1, source_target_pairs={{1,2},{3,4},{5,6},{7,0},{2,1},{4,3},{6,5},{0,7},{9,10},{11,12},{13... | collective-permute-start | bytes 1179656 | tf_op jit(solution)/shard_map/ppermute | solution.py:337
  78.4 43.8 %collective-permute-start.28 = (bf16[384,768]{1,0:T(8,128)(2,1)S(1)}, bf16[384,768]{1,0:T(8,128)(2,1)}, u32[]{:S(2)}, u32[]{:S(2)}) collective-permute-start(bf16[384,768]{1,0:T(8,128)(2,1)S(1)} %bitcast_select_fusion.own_ref), channel_id=1, source_target_pairs={{0,1},{2,3},{4,5},{6,7},{1,0},{3,2},{5,4},{7,6},{8,9},{10,11},{12,... | collective-permute-start | bytes 1769480 | tf_op jit(solution)/shard_map/ppermute | solution.py:313
  81.1 26.2 %collective-permute-start.12 = (bf16[2,2,64,768]{3,2,1,0:T(8,128)(2,1)}, bf16[2,2,64,768]{3,2,1,0:T(8,128)(2,1)}, u32[]{:S(2)}, u32[]{:S(2)}) collective-permute-start(bf16[2,2,64,768]{3,2,1,0:T(8,128)(2,1)} %pad_maximum_fusion), channel_id=1, source_target_pairs={{0,1},{2,3},{4,5},{6,7},{1,0},{3,2},{5,4},{7,6},{8,9},{10,11},{12,... | collective-permute-start | bytes 1179656 | tf_op jit(solution)/shard_map/ppermute | solution.py:344
  81.1 26.2 %collective-permute-start.13 = (bf16[2,2,64,768]{3,2,1,0:T(8,128)(2,1)}, bf16[2,2,64,768]{3,2,1,0:T(8,128)(2,1)}, u32[]{:S(2)}, u32[]{:S(2)}) collective-permute-start(bf16[2,2,64,768]{3,2,1,0:T(8,128)(2,1)} %pad_maximum_fusion), channel_id=1, source_target_pairs={{1,2},{3,4},{5,6},{7,0},{2,1},{4,3},{6,5},{0,7},{9,10},{11,12},{13... | collective-permute-start | bytes 1179656 | tf_op jit(solution)/shard_map/ppermute | solution.py:343
  83.2 8.0 %collective-permute-start.16 = (f32[1,16,128]{2,1,0:T(8,128)S(1)}, f32[1,16,128]{2,1,0:T(8,128)S(1)}, u32[]{:S(2)}, u32[]{:S(2)}) collective-permute-start(f32[1,16,128]{2,1,0:T(8,128)S(1)} %get-tuple-element.30), channel_id=1, source_target_pairs={{0,8},{16,24},{8,0},{24,16},{1,9},{17,25},{9,1},{25,17},{2,10},{18... | collective-permute-start | bytes 24584 | tf_op jit(solution)/shard_map/ppermute | solution.py:338
  88.4 6.4 %collective-permute-start.17 = (f32[1,16,128]{2,1,0:T(8,128)S(1)}, f32[1,16,128]{2,1,0:T(8,128)S(1)}, u32[]{:S(2)}, u32[]{:S(2)}) collective-permute-start(f32[1,16,128]{2,1,0:T(8,128)S(1)} %get-tuple-element.29), channel_id=1, source_target_pairs={{8,16},{16,8},{9,17},{17,9},{10,18},{18,10},{11,19},{19,11},{12,20... | collective-permute-start | bytes 24584 | tf_op jit(solution)/shard_map/ppermute | solution.py:339
  91.1 4.4 %collective-permute-start.14 = (f32[1,2,16,128]{3,2,1,0:T(8,128)S(1)}, f32[1,2,16,128]{3,2,1,0:T(8,128)S(1)}, u32[]{:S(2)}, u32[]{:S(2)}) collective-permute-start(f32[1,2,16,128]{3,2,1,0:T(8,128)S(1)} %copy-done.18), channel_id=1, source_target_pairs={{0,1},{2,3},{4,5},{6,7},{1,0},{3,2},{5,4},{7,6},{8,9},{10,11},{12,... | collective-permute-start | bytes 49160 | tf_op jit(solution)/shard_map/ppermute | solution.py:340
  94.9 5.0 %collective-permute-start.15 = (f32[1,2,16,128]{3,2,1,0:T(8,128)S(1)}, f32[1,2,16,128]{3,2,1,0:T(8,128)S(1)}, u32[]{:S(2)}, u32[]{:S(2)}) collective-permute-start(f32[1,2,16,128]{3,2,1,0:T(8,128)S(1)} %copy-done.18), channel_id=1, source_target_pairs={{1,2},{3,4},{5,6},{7,0},{2,1},{4,3},{6,5},{0,7},{9,10},{11,12},{13... | collective-permute-start | bytes 49160 | tf_op jit(solution)/shard_map/ppermute | solution.py:337
  95.6 11.7 %collective-permute-start.18 = (f32[2,1,16,128]{3,2,1,0:T(8,128)S(1)}, f32[2,1,16,128]{3,2,1,0:T(8,128)S(1)}, u32[]{:S(2)}, u32[]{:S(2)}) collective-permute-start(f32[2,1,16,128]{3,2,1,0:T(8,128)S(1)} %pad_maximum_fusion.1), channel_id=1, source_target_pairs={{0,1},{2,3},{4,5},{6,7},{1,0},{3,2},{5,4},{7,6},{8,9},{10,11},{12,... | collective-permute-start | bytes 49160 | tf_op jit(solution)/shard_map/ppermute | solution.py:344
  99.8 7.5 %collective-permute-start.19 = (f32[2,1,16,128]{3,2,1,0:T(8,128)S(1)}, f32[2,1,16,128]{3,2,1,0:T(8,128)S(1)}, u32[]{:S(2)}, u32[]{:S(2)}) collective-permute-start(f32[2,1,16,128]{3,2,1,0:T(8,128)S(1)} %pad_maximum_fusion.1), channel_id=1, source_target_pairs={{1,2},{3,4},{5,6},{7,0},{2,1},{4,3},{6,5},{0,7},{9,10},{11,12},{13... | collective-permute-start | bytes 49160 | tf_op jit(solution)/shard_map/ppermute | solution.py:343
  (22 other events, 227.8 us)
